TPU v7x, 512 devices: a whole 4x4x16 slice. The times are simulated.
512 devices in a mesh: section: 4 (over x), space: 128 (over y, z, core).
Axes of the slice: x: 4, y: 4, z: 16, core: 2. Of those that a mesh axis runs over, the one named last changes fastest.
Arguments:
- feats: bfloat16 [4, 96, 196608], P('section', None, 'space'), may hold values from -6 to 6
- mask: int32 [4, 196608], P('section', 'space'), may hold values 0 or 1
- conv_w: bfloat16 [4, 27, 96, 96], P('section'), may hold values from -0.125 to 0.125
- rules: int32 [4, 384, 26], P('section', 'space'), may hold values from 0 to 5
- send_lists: int32 [4, 128, 2, 1], P('section', 'space'), may hold values from 0 to 2
- pool_map: int32 [4, 384, 8], P('section', 'space'), may hold values from 0 to 3, as said below
- send_order: int32 [4, 128, 1536], P('section', 'space'), may hold values from 0 to 1535, each once within a row
- patch_order: int32 [4, 128, 1536], P('section', 'space'), may hold values from 0 to 1535, each once within a row
- ln_gain: bfloat16 [4, 96], P('section'), may hold values from 0.099609375 to 1.8984375
- w_query: bfloat16 [4, 96, 96], P('section'), may hold values from -5 to 5
- w_key: bfloat16 [4, 96, 96], P('section'), may hold values from -5 to 5
- w_value: bfloat16 [4, 96, 96], P('section'), may hold values from -0.625 to 0.625
- w_out: bfloat16 [4, 96, 96], P('section'), may hold values from -0.625 to 0.625
Outputs:
- result: bfloat16 [4, 96, 196608], P('section', None, 'space')
Inputs may be any that keep to these rules, and one draw needn't show every extreme that they name: `pool_map`: in the rows of one space index, each of the numbers 0 to 2 appears exactly once; every other entry is 3, an empty octant.
All inputs are finite; a program needn't handle non-finite values. No bound on the sum of `mask` on one device may be relied on, other than what follows from the above.
Results may differ from a plain program's by a relative error of at most 0.005.
Values may be sent and summed in bfloat16 or wider, within the bound.
No kernel may reach another device: no remote copies, remote signals or barrier semaphores. Data moves between devices by JAX's collectives and lax.ppermute only.
A program may use at most 64 MiB of HBM per device.

v0:
```python
import math

import jax
import jax.numpy as jnp
import numpy as np
from jax import lax
from jax.sharding import PartitionSpec as P

HEADS = 6
HEAD_DIM = 16
EDGE = 8
PATCH = 384


EPSILON = 1e-05
MASK_FILL = -1e30


def shifted(block, axis, distance):
    devices = range(lax.axis_size(axis))
    route = [(i - distance, i) for i in devices if i - distance in devices]
    return lax.ppermute(block, axis, route)


def offset_tables(edge_cells):
    padded_side = edge_cells + 2
    coords = np.arange(padded_side) - 1
    grid_x, grid_y, grid_z = np.meshgrid(coords, coords, coords, indexing="ij")

    def direction(grid):
        return np.where(grid < 0, 0, np.where(grid >= edge_cells, 2, 1))

    offset = direction(grid_x) * 9 + direction(grid_y) * 3 + direction(grid_z)
    source = (
        np.mod(grid_x, edge_cells) * edge_cells + np.mod(grid_y, edge_cells)
    ) * edge_cells + np.mod(grid_z, edge_cells)
    inner_range = np.arange(edge_cells)
    inner_x, inner_y, inner_z = np.meshgrid(inner_range, inner_range, inner_range, indexing="ij")
    half_edge = edge_cells // 2
    octant = (inner_x // half_edge * 4 + inner_y // half_edge * 2 + inner_z // half_edge).reshape(
        -1
    )
    within = (
        (inner_x % half_edge * half_edge + inner_y % half_edge) * half_edge + inner_z % half_edge
    ).reshape(-1)
    lowest = np.minimum(np.minimum(inner_x, inner_y), inner_z)
    highest = np.maximum(np.maximum(inner_x, inner_y), inner_z)
    on_surface = ((lowest == 0) | (highest == edge_cells - 1)).reshape(-1)
    surface_index = np.arange(edge_cells**3)[on_surface]
    return (
        offset.reshape(-1).astype(np.int32),
        source.reshape(-1).astype(np.int32),
        octant.astype(np.int32),
        within.astype(np.int32),
        surface_index.astype(np.int32),
    )


def attend(serial, serial_mask, norm_gain, query_weight, key_weight, value_weight):
    tok_count = serial.shape[1]
    float_values = serial.astype(jnp.float32)
    center = jnp.mean(float_values, axis=0, keepdims=True)
    variance = jnp.mean((float_values - center) ** 2, axis=0, keepdims=True)
    normed = (
        (float_values - center)
        * lax.rsqrt(variance + EPSILON)
        * norm_gain.astype(jnp.float32)[:, None]
    ).astype(jnp.bfloat16)
    stacked = jnp.concatenate([query_weight, key_weight, value_weight], axis=0)
    projected = jnp.dot(stacked, normed, preferred_element_type=jnp.float32).astype(jnp.bfloat16)
    groups = tok_count // (2 * PATCH)
    shaped = projected.reshape(3, HEADS, HEAD_DIM, groups, 2, PATCH).transpose(3, 0, 4, 1, 2, 5)
    key_flags = serial_mask.reshape(groups, 2, PATCH)
    score_scale = 1.0 / math.sqrt(HEAD_DIM)
    diagonal = jnp.eye(PATCH, dtype=bool)[None, None]

    def one_group(group_items):
        pieces, flags_here = group_items
        scores = (
            jnp.einsum("phdq,phdk->phqk", pieces[0], pieces[1], preferred_element_type=jnp.float32)
            * score_scale
        )
        visible = (flags_here[:, None, None, :] > 0) | diagonal
        scores = jnp.where(visible, scores, MASK_FILL)
        row_max = jnp.max(scores, axis=-1, keepdims=True)
        exponent = jnp.exp(scores - row_max)
        row_total = jnp.sum(exponent, axis=-1, keepdims=True)
        weights = (exponent / row_total).astype(jnp.bfloat16)
        return jnp.einsum(
            "phqk,phdk->phdq", weights, pieces[2], preferred_element_type=jnp.float32
        ).astype(jnp.bfloat16)

    outputs = lax.map(one_group, (shaped, key_flags))
    return outputs.transpose(2, 3, 0, 1, 4).reshape(HEADS * HEAD_DIM, tok_count)


def shards(
    feats,
    mask,
    conv_w,
    rules,
    send_lists,
    pool_map,
    send_order,
    patch_order,
    ln_gain,
    w_query,
    w_key,
    w_value,
    w_out,
):
    channels = feats.shape[1]
    tok_count = feats.shape[2]
    voxels = EDGE**3
    blk_count = tok_count // voxels
    half_edge = EDGE // 2
    coarse = half_edge**3
    side = EDGE + 2
    spaces = lax.axis_size("space")
    pair_count = tok_count // spaces
    offset, source, octant, within, surface_index = offset_tables(EDGE)
    active = mask[0]
    active_float = active.astype(jnp.float32)
    masked = feats[0] * active.astype(jnp.bfloat16)
    blocks = masked.reshape(channels, blk_count, voxels)
    received = []
    for row_index, direction_step in ((1, 1), (0, -1)):
        outgoing = jnp.take(blocks, send_lists[0, 0, row_index], axis=1)
        whole_blocks = shifted(outgoing, "space", direction_step)
        received.append(whole_blocks)
    block_table = jnp.concatenate(
        [blocks, received[0], received[1], jnp.zeros((channels, 1, voxels), jnp.bfloat16)], axis=1
    ).reshape(channels, -1)
    local_ids = jnp.arange(blk_count, dtype=jnp.int32)
    rule_rows = rules[0]
    neighbor = jnp.concatenate([rule_rows[:, :13], local_ids[:, None], rule_rows[:, 13:]], axis=1)
    gather_index = (
        neighbor[:, jnp.asarray(offset)] * voxels + jnp.asarray(source)[None, :]
    ).astype(jnp.int32)
    padded = jnp.take(block_table, gather_index.reshape(-1), axis=1).reshape(
        channels, blk_count, side, side, side
    )
    conv_sum = jnp.zeros((channels, tok_count), jnp.float32)
    for shift_x in range(3):
        stacked_views = jnp.concatenate(
            [
                padded[
                    :,
                    :,
                    shift_x : shift_x + EDGE,
                    shift_y : shift_y + EDGE,
                    shift_z : shift_z + EDGE,
                ].reshape(channels, tok_count)
                for shift_y in range(3)
                for shift_z in range(3)
            ],
            axis=0,
        )
        weight_rows = (
            conv_w[0, shift_x * 9 : (shift_x + 1) * 9]
            .transpose(1, 0, 2)
            .reshape(channels, 9 * channels)
        )
        conv_sum = conv_sum + jnp.dot(
            weight_rows, stacked_views, preferred_element_type=jnp.float32
        )
    conv_out = conv_sum * active_float[None, :]
    pooled = (
        conv_out.reshape(channels, blk_count, half_edge, 2, half_edge, 2, half_edge, 2)
        .mean(axis=(3, 5, 7))
        .reshape(channels, blk_count * coarse)
        .astype(jnp.bfloat16)
    )
    coarser = shifted(pooled, "section", 1)
    child_table = jnp.concatenate(
        [
            coarser.reshape(channels, blk_count, coarse),
            jnp.zeros((channels, 1, coarse), jnp.bfloat16),
        ],
        axis=1,
    ).reshape(channels, -1)
    lift_index = (
        pool_map[0][:, jnp.asarray(octant)] * coarse + jnp.asarray(within)[None, :]
    ).astype(jnp.int32)
    lifted = jnp.take(child_table, lift_index.reshape(-1), axis=1)
    hidden = (
        (masked.astype(jnp.float32) + conv_out + lifted.astype(jnp.float32)) * active_float[None, :]
    ).astype(jnp.bfloat16)
    order_out = send_order[0, 0]
    order_in = patch_order[0, 0]
    outbound = jnp.take(hidden, order_out, axis=1).reshape(channels, spaces, pair_count)
    outbound_mask = jnp.take(active.astype(jnp.bfloat16), order_out).reshape(1, spaces, pair_count)
    inbound, inbound_mask = (
        lax.all_to_all(outbound, "space", split_axis=1, concat_axis=1, tiled=True),
        lax.all_to_all(outbound_mask, "space", split_axis=1, concat_axis=1, tiled=True),
    )
    serial = jnp.take(inbound.reshape(channels, tok_count), order_in, axis=1)
    serial_mask = jnp.take(inbound_mask.reshape(tok_count), order_in)
    attended = attend(serial, serial_mask, ln_gain[0], w_query[0], w_key[0], w_value[0])
    owner_slots = (
        jnp.zeros_like(attended).at[:, order_in].set(attended).reshape(channels, spaces, pair_count)
    )
    returned = lax.all_to_all(owner_slots, "space", split_axis=1, concat_axis=1, tiled=True)
    home_rows = jnp.zeros_like(attended).at[:, order_out].set(returned.reshape(channels, tok_count))
    result = (
        (
            hidden.astype(jnp.float32)
            + jnp.dot(w_out[0], home_rows, preferred_element_type=jnp.float32)
        )
        * active_float[None, :]
    ).astype(jnp.bfloat16)
    return result[None]


def solution(mesh):
    placed = (
        P("section", None, "space"),
        P("section", "space"),
        P("section", None, None, None),
        P("section", "space", None),
        P("section", "space", None, None),
        P("section", "space", None),
        P("section", "space", None),
        P("section", "space", None),
        P("section", None),
        P("section", None, None),
        P("section", None, None),
        P("section", None, None),
        P("section", None, None),
    )
    return jax.shard_map(
        shards, mesh=mesh, in_specs=placed, out_specs=P("section", None, "space"), check_vma=False
    )
```

profile of v0, /device:TPU:1, one launch (start us, length us, event | category | flops | bytes accessed | tf_op | source)
XLA Modules:
  0.0 232.9 jit_solution(348382900659733629)
XLA Ops:
  7.6 4.9 %collective-permute-start = (bf16[96,1,512]{2,1,0:T(2,128)(2,1)S(1)}, bf16[96,1,512]{2,1,0:T(2,128)(2,1)S(1)}, u32[]{:S(2)}, u32[]{:S(2)}) collective-permute-start(bf16[96,1,512]{2,1,0:T(2,128)(2,1)S(1)} %get-tuple-element.101), channel_id=1, source_target_pairs={{0,1},{1,2},{2,3},{3,4},{4,5},{5,6},{6,7},{7,8},{8,9},{9,10},{10,1... | collective-permute-start | bytes 294920 | tf_op jit(solution)/shard_map/ppermute | solution.py:22
  12.5 5.1 %collective-permute-start.1 = (bf16[96,1,512]{2,1,0:T(2,128)(2,1)S(1)}, bf16[96,1,512]{2,1,0:T(2,128)(2,1)S(1)}, u32[]{:S(2)}, u32[]{:S(2)}) collective-permute-start(bf16[96,1,512]{2,1,0:T(2,128)(2,1)S(1)} %get-tuple-element.102), channel_id=1, source_target_pairs={{1,0},{2,1},{3,2},{4,3},{5,4},{6,5},{7,6},{8,7},{9,8},{10,9},{11,1... | collective-permute-start | bytes 294920 | tf_op jit(solution)/shard_map/ppermute | solution.py:22
  18.4 9.5 %gather_fusion.6 = bf16[1536]{0:T(1024)(128)(2,1)S(1)} fusion(bf16[1536]{0:T(1024)(128)(2,1)S(1)} %convert_reduce_fusion.2, s32[2048]{0:T(1024)S(1)} %pad_clamp_fusion.2), kind=kCustom, calls=%fused_computation.1.clone | custom fusion | bytes 12288 | tf_op jit(solution)/shard_map/jit(_take)/gather | solution.py:192
  28.7 17.3 %all-to-all-start.1 = ((bf16[1,128,12]{2,0,1:T(2,128)(2,1)}), bf16[1,128,12]{2,0,1:T(2,128)(2,1)S(1)}, u32[]{:S(2)}, u32[]{:S(2)}) async-start(bf16[1,128,12]{2,0,1:T(2,128)(2,1)} %reshape.571), calls=%async_computation.1 | async-start | bytes 131072 | tf_op jit(solution)/shard_map/all_to_all | solution.py:195
  56.1 9.3 %gather_fusion.1 = bf16[3000,96]{1,0:T(8,128)(2,1)S(1)} fusion(bf16[96,3072]{0,1:T(8,128)(2,1)S(1)} %bitcast.185, s32[3072]{0:T(1024)S(1)} %pad_clamp_fusion), kind=kCustom, calls=%fused_computation.5 | custom fusion | bytes 1164000 | tf_op jit(solution)/shard_map/jit(_take)/gather | solution.py:140
  66.6 4.0 %fusion.56 = (bf16[96,3,8,8,8]{0,4,3,2,1:T(8,128)(2,1)}, bf16[96,3,8,8,8]{0,4,3,2,1:T(8,128)(2,1)}, bf16[96,3,8,8,8]{0,4,3,2,1:T(8,128)(2,1)}, bf16[96,3,8,8,8]{...) fusion(bf16[96,3,10,10,10]{0,4,3,2,1:T(8,128)(2,1)S(1)} %broadc, ...), kind=kLoop, calls=%fused_computation.120 | loop fusion | bytes 11206656 | tf_op jit(solution)/shard_map/slice | solution.py:147
  72.4 4.4 %concatenate.23 = bf16[864,1536]{0,1:T(8,128)(2,1)S(1)} concatenate(bf16[96,1536]{0,1:T(8,128)(2,1)} %bitcast.195, bf16[96,1536]{0,1:T(8,128)(2,1)} %bitcast.194, bf16[96,1536]{0,1:T(8,128)(2,1)} %bitcast.193, bf16[96,1536]{0,1:T(8,128)(2,1)} %bitcast.192, bf16[96,1536]{0,1:T(8,128)(2,1)} %bitcast.191, bf16[96,1536]{0,1:T(8,128)(2,1)} %bitcast.190, bf16[96,1536]{0,1:T(8,128)(2,1)} %bitcast.189, ...), dimensions={0} | concatenate | bytes 5308416 | tf_op jit(solution)/shard_map/concatenate | solution.py:145
  78.7 4.5 %concatenate.24 = bf16[864,1536]{0,1:T(8,128)(2,1)S(1)} concatenate(bf16[96,1536]{0,1:T(8,128)(2,1)} %bitcast.213, bf16[96,1536]{0,1:T(8,128)(2,1)} %bitcast.212, bf16[96,1536]{0,1:T(8,128)(2,1)} %bitcast.211, bf16[96,1536]{0,1:T(8,128)(2,1)} %bitcast.210, bf16[96,1536]{0,1:T(8,128)(2,1)} %bitcast.209, bf16[96,1536]{0,1:T(8,128)(2,1)} %bitcast.208, bf16[96,1536]{0,1:T(8,128)(2,1)} %bitcast.207, ...), dimensions={0} | concatenate | bytes 5308416 | tf_op jit(solution)/shard_map/concatenate | solution.py:145
  85.9 4.5 %concatenate.25 = bf16[864,1536]{0,1:T(8,128)(2,1)S(1)} concatenate(bf16[96,1536]{0,1:T(8,128)(2,1)} %bitcast.204, bf16[96,1536]{0,1:T(8,128)(2,1)} %bitcast.203, bf16[96,1536]{0,1:T(8,128)(2,1)} %bitcast.202, bf16[96,1536]{0,1:T(8,128)(2,1)} %bitcast.201, bf16[96,1536]{0,1:T(8,128)(2,1)} %bitcast.200, bf16[96,1536]{0,1:T(8,128)(2,1)} %bitcast.199, bf16[96,1536]{0,1:T(8,128)(2,1)} %bitcast.198, ...), dimensions={0} | concatenate | bytes 5308416 | tf_op jit(solution)/shard_map/concatenate | solution.py:145
  97.8 3.2 %gather_fusion.3 = bf16[1536,96]{1,0:T(8,128)(2,1)S(1)} fusion(bf16[96,256]{0,1:T(8,128)(2,1)S(1)} %bitcast.184, s32[2048]{0:T(1024)S(1)} %pad_clamp_fusion.3), kind=kCustom, calls=%fused_computation.7 | custom fusion | bytes 595968 | tf_op jit(solution)/shard_map/jit(_take)/gather | solution.py:185
  101.7 3.2 %gather_fusion.4 = bf16[1536,96]{1,0:T(8,128)(2,1)S(1)} fusion(bf16[96,1536]{0,1:T(8,128)(2,1)S(1)} %copy.75, s32[2048]{0:T(1024)S(1)} %pad_clamp_fusion.2), kind=kCustom, calls=%fused_computation.clone | custom fusion | bytes 595968 | tf_op jit(solution)/shard_map/jit(_take)/gather | solution.py:191
  106.1 17.0 %all-to-all-start = ((bf16[96,128,12]{0,2,1:T(8,128)(2,1)}), bf16[96,128,12]{0,2,1:T(8,128)(2,1)S(1)}, u32[]{:S(2)}, u32[]{:S(2)}) async-start(bf16[96,128,12]{0,2,1:T(8,128)(2,1)} %reshape.412), calls=%async_computation | async-start | bytes 1048576 | tf_op jit(solution)/shard_map/all_to_all | solution.py:194
  123.6 9.5 %gather_fusion.7 = bf16[1536]{0:T(1024)(128)(2,1)S(1)} fusion(bf16[1536]{0:T(1024)(128)(2,1)S(1)} %reshape.416, s32[2048]{0:T(1024)S(1)} %pad_clamp_fusion.1), kind=kCustom, calls=%fused_computation.3.clone | custom fusion | bytes 12288 | tf_op jit(solution)/shard_map/jit(_take)/gather | solution.py:198
  133.1 23.2 %all-to-all-done = bf16[96,128,12]{0,2,1:T(8,128)(2,1)S(1)} async-done(((bf16[96,128,12]{0,2,1:T(8,128)(2,1)}), bf16[96,128,12]{0,2,1:T(8,128)(2,1)S(1)}, u32[]{:S(2)}, u32[]{:S(2)}) %all-to-all-start) | async-done | bytes 294944 | tf_op jit(solution)/shard_map/all_to_all | solution.py:194
  156.5 3.2 %gather_fusion.5 = bf16[1536,96]{1,0:T(8,128)(2,1)S(1)} fusion(bf16[96,1536]{0,1:T(8,128)(2,1)S(1)} %reshape.413, s32[2048]{0:T(1024)S(1)} %pad_clamp_fusion.1), kind=kCustom, calls=%fused_computation.2.clone | custom fusion | bytes 595968 | tf_op jit(solution)/shard_map/jit(_take)/gather | solution.py:197
  163.7 16.9 %while.12 = (s32[]{:T(128)}, bf16[2,2,6,16,384]{4,3,2,1,0:T(8,128)(2,1)S(1)}, bf16[2,3,2,6,16,384]{5,4,3,2,1,0:T(8,128)(2,1)S(1)}, bf16[2,2,384]{2,1,0:T(2,128)(2,1)S(1)}, s32[]{:T(128)}, /*index=5*/s32[]{:T(128)}, s32[]{}, s32[]{}) while((s32[]{:T(128)}, bf16[2,2,6,16,384]{4,3,2,1,0:T(8,128)(2,1)S(1)}, ...), condition=%wide.region_6.10_spmd.clone, body=%wide.region_3.0_spmd.clone.sunk | while | flops 124380288 | bytes 15678585 | solution.py:93
  164.0 4.5 %fusion.72 = (f32[2,6,384]{2,1,0:T(8,128)S(1)}, f32[2,6,384,384]{2,3,1,0:T(8,128)}) fusion(pred[2,384,384]{1,2,0:T(8,128)(4,1)S(1)} %broadcast_or_fusion.2, bf16[2,3,2,6,16,384]{5,4,3,2,1,0:T(8,128)(2,1)S(1)} %get-tuple-element.154, s32[]{:T(128)} %get-tuple-element.144, s32[]{:T(128)S(6)} %add.310), kind=kOutput, calls=%fused_computation.119.clone.1 | convolution fusion | flops 63701376 | bytes 7687172 | tf_op jit(solution)/shard_map/while/body/eval_jaxpr/sub | solution.py:86
  168.5 3.7 %fusion.73 = bf16[2,2,6,16,384]{4,3,2,1,0:T(8,128)(2,1)S(1)} fusion(bf16[2,2,6,16,384]{4,3,2,1,0:T(8,128)(2,1)S(1)} %get-tuple-element.145, s32[]{:T(128)} %get-tuple-element.144, f32[2,6,384,384]{2,3,1,0:T(8,128)} %get-tuple-element.134, f32[2,6,384]{2,1,0:T(8,128)S(1)} %get-tuple-element.135, ...), kind=kOutput, calls=%fused_computation.22.clone.1 | convolution fusion | flops 60235776 | bytes 7398404 | tf_op jit(solution)/shard_map/while/body/eval_jaxpr/phqk,phdk->phdq/dot_general | solution.py:89
  172.5 4.5 %fusion.72 = (f32[2,6,384]{2,1,0:T(8,128)S(1)}, f32[2,6,384,384]{2,3,1,0:T(8,128)}) fusion(pred[2,384,384]{1,2,0:T(8,128)(4,1)S(1)} %broadcast_or_fusion.2, bf16[2,3,2,6,16,384]{5,4,3,2,1,0:T(8,128)(2,1)S(1)} %get-tuple-element.154, s32[]{:T(128)} %get-tuple-element.144, s32[]{:T(128)S(6)} %add.310), kind=kOutput, calls=%fused_computation.119.clone.1 | convolution fusion | flops 63701376 | bytes 7687172 | tf_op jit(solution)/shard_map/while/body/eval_jaxpr/sub | solution.py:86
  177.0 3.7 %fusion.73 = bf16[2,2,6,16,384]{4,3,2,1,0:T(8,128)(2,1)S(1)} fusion(bf16[2,2,6,16,384]{4,3,2,1,0:T(8,128)(2,1)S(1)} %get-tuple-element.145, s32[]{:T(128)} %get-tuple-element.144, f32[2,6,384,384]{2,3,1,0:T(8,128)} %get-tuple-element.134, f32[2,6,384]{2,1,0:T(8,128)S(1)} %get-tuple-element.135, ...), kind=kOutput, calls=%fused_computation.22.clone.1 | convolution fusion | flops 60235776 | bytes 7398404 | tf_op jit(solution)/shard_map/while/body/eval_jaxpr/phqk,phdk->phdq/dot_general | solution.py:89
  181.3 4.6 %scatter_custom_fusion = bf16[96,1536]{0,1:T(8,128)(2,1)S(1)} fusion(s32[1536]{0:T(1024)S(1)} %fusion.53, bf16[1536,96]{1,0:T(8,128)(2,1)S(1)} %copy.79, bf16[]{:T(256)} %constant.72.clone.1), kind=kCustom, calls=%fused_computation.79 | custom fusion | bytes 294914 | tf_op jit(solution)/shard_map/scatter | solution.py:201
  186.8 7.1 %all-to-all-start.2 = ((bf16[96,128,12]{0,2,1:T(8,128)(2,1)}), bf16[96,128,12]{0,2,1:T(8,128)(2,1)S(1)}, u32[]{:S(2)}, u32[]{:S(2)}) async-start(bf16[96,128,12]{0,2,1:T(8,128)(2,1)} %reshape.419), calls=%async_computation.2 | async-start | bytes 1048576 | tf_op jit(solution)/shard_map/all_to_all | solution.py:203
  194.0 33.2 %all-to-all-done.2 = bf16[96,128,12]{0,2,1:T(8,128)(2,1)S(1)} async-done(((bf16[96,128,12]{0,2,1:T(8,128)(2,1)}), bf16[96,128,12]{0,2,1:T(8,128)(2,1)S(1)}, u32[]{:S(2)}, u32[]{:S(2)}) %all-to-all-start.2) | async-done | bytes 294944 | tf_op jit(solution)/shard_map/all_to_all | solution.py:203
  227.3 4.5 %scatter_custom_fusion.1 = bf16[96,1536]{0,1:T(8,128)(2,1)S(1)} fusion(s32[1536]{0:T(1024)S(1)} %fusion.52, bf16[96,1536]{0,1:T(8,128)(2,1)S(1)} %reshape.550, bf16[]{:T(256)} %constant.72.clone.1), kind=kCustom, calls=%fused_computation.61 | custom fusion | bytes 688130 | tf_op jit(solution)/shard_map/scatter | solution.py:204
  (127 shorter events, 39.8 us)
Async XLA Ops:
  0.0 231.9 %copy-start = (bf16[1,96,96]{2,1,0:T(8,128)(2,1)S(1)}, bf16[1,96,96]{2,1,0:T(8,128)(2,1)}, u32[]{:S(2)}) copy-start(bf16[1,96,96]{2,1,0:T(8,128)(2,1)} %param.37) | copy-start | bytes 55300
  7.0 38.9 %copy-start.4 = (s32[1,1536]{1,0:T(1,128)S(1)}, s32[1,1536]{1,0:T(1,128)}, u32[]{:S(2)}) copy-start(s32[1,1536]{1,0:T(1,128)} %param.26) | copy-start | bytes 18436
  7.0 39.0 %copy-start.11 = (s32[1,3,26]{2,0,1:T(1,128)S(1)}, s32[1,3,26]{2,0,1:T(1,128)}, u32[]{:S(2)}) copy-start(s32[1,3,26]{2,0,1:T(1,128)} %param.28) | copy-start | bytes 940
  7.1 39.2 %copy-start.8 = (s32[1000]{0:T(1024)S(1)}, s32[1000]{0:T(1024)}, u32[]{:S(2)}) copy-start(s32[1000]{0:T(1024)} %constant.172) | copy-start | bytes 12004
  7.6 47.1 %collective-permute-start = (bf16[96,1,512]{2,1,0:T(2,128)(2,1)S(1)}, bf16[96,1,512]{2,1,0:T(2,128)(2,1)S(1)}, u32[]{:S(2)}, u32[]{:S(2)}) collective-permute-start(bf16[96,1,512]{2,1,0:T(2,128)(2,1)S(1)} %get-tuple-element.101), channel_id=1, source_target_pairs={{0,1},{1,2},{2,3},{3,4},{4,5},{5,6},{6,7},{7,8},{8,9},{9,10},{10,1... | collective-permute-start | bytes 294920 | tf_op jit(solution)/shard_map/ppermute | solution.py:22
  12.5 42.2 %collective-permute-start.1 = (bf16[96,1,512]{2,1,0:T(2,128)(2,1)S(1)}, bf16[96,1,512]{2,1,0:T(2,128)(2,1)S(1)}, u32[]{:S(2)}, u32[]{:S(2)}) collective-permute-start(bf16[96,1,512]{2,1,0:T(2,128)(2,1)S(1)} %get-tuple-element.102), channel_id=1, source_target_pairs={{1,0},{2,1},{3,2},{4,3},{5,4},{6,5},{7,6},{8,7},{9,8},{10,9},{11,1... | collective-permute-start | bytes 294920 | tf_op jit(solution)/shard_map/ppermute | solution.py:22
  18.4 31.1 %copy-start.7 = (s32[1000]{0:T(1024)S(1)}, s32[1000]{0:T(1024)}, u32[]{:S(2)}) copy-start(s32[1000]{0:T(1024)} %constant.99.clone) | copy-start | bytes 12004
  18.4 31.3 %copy-start.2 = (bf16[1,27,96,96]{3,2,1,0:T(8,128)(2,1)S(1)}, bf16[1,27,96,96]{3,2,1,0:T(8,128)(2,1)}, u32[]{:S(2)}) copy-start(bf16[1,27,96,96]{3,2,1,0:T(8,128)(2,1)} %param.27) | copy-start | bytes 1492996
  27.9 25.2 %copy-start.10 = (s32[512]{0:T(512)S(1)}, s32[512]{0:T(512)}, u32[]{:S(2)}) copy-start(s32[512]{0:T(512)} %constant.173) | copy-start | bytes 6148
  27.9 26.2 %copy-start.9 = (s32[512]{0:T(512)S(1)}, s32[512]{0:T(512)}, u32[]{:S(2)}) copy-start(s32[512]{0:T(512)} %constant.123.clone) | copy-start | bytes 6148
  28.7 77.4 %all-to-all-start.1 = ((bf16[1,128,12]{2,0,1:T(2,128)(2,1)}), bf16[1,128,12]{2,0,1:T(2,128)(2,1)S(1)}, u32[]{:S(2)}, u32[]{:S(2)}) async-start(bf16[1,128,12]{2,0,1:T(2,128)(2,1)} %reshape.571), calls=%async_computation.1 | async-start | bytes 131072 | tf_op jit(solution)/shard_map/all_to_all | solution.py:195
  49.2 5.3 %copy-start.3 = (s32[10,10,10]{2,1,0:T(8,128)S(1)}, s32[10,10,10]{2,1,0:T(8,128)}, u32[]{:S(2)}) copy-start(s32[10,10,10]{2,1,0:T(8,128)} %constant.163) | copy-start | bytes 12004
  92.6 8.6 %copy-start.1 = (bf16[1,96,1536]{2,1,0:T(8,128)(2,1)S(1)}, bf16[1,96,1536]{2,1,0:T(8,128)(2,1)}, u32[]{:S(2)}) copy-start(bf16[1,96,1536]{2,1,0:T(8,128)(2,1)} %param.25) | copy-start | bytes 884740
  93.5 4.3 %collective-permute-start.2 = (bf16[96,192]{0,1:T(8,128)(2,1)S(1)}, bf16[96,192]{0,1:T(8,128)(2,1)S(1)}, u32[]{:S(2)}, u32[]{:S(2)}) collective-permute-start(bf16[96,192]{0,1:T(8,128)(2,1)S(1)} %bitcast.226), channel_id=1, source_target_pairs={{0,128},{128,256},{256,384},{1,129},{129,257},{257,385},{2,130},{1... | collective-permute-start | bytes 110600 | tf_op jit(solution)/shard_map/ppermute | solution.py:22
  101.6 21.5 %copy-start.5 = (s32[1,1,1536]{2,1,0:T(1,128)S(1)}, s32[1,1,1536]{2,1,0:T(1,128)}, u32[]{:S(2)}) copy-start(s32[1,1,1536]{2,1,0:T(1,128)} %param.32) | copy-start | bytes 18436
  101.6 21.6 %copy-start.15 = (bf16[1,96]{1,0:T(2,128)(2,1)S(1)}, bf16[1,96]{1,0:T(2,128)(2,1)}, u32[]{:S(2)}) copy-start(bf16[1,96]{1,0:T(2,128)(2,1)} %param.33) | copy-start | bytes 580
  106.1 50.3 %all-to-all-start = ((bf16[96,128,12]{0,2,1:T(8,128)(2,1)}), bf16[96,128,12]{0,2,1:T(8,128)(2,1)S(1)}, u32[]{:S(2)}, u32[]{:S(2)}) async-start(bf16[96,128,12]{0,2,1:T(8,128)(2,1)} %reshape.412), calls=%async_computation | async-start | bytes 1048576 | tf_op jit(solution)/shard_map/all_to_all | solution.py:194
  133.0 28.5 %copy-start.12 = (bf16[1,96,96]{2,1,0:T(8,128)(2,1)S(1)}, bf16[1,96,96]{2,1,0:T(8,128)(2,1)}, u32[]{:S(2)}) copy-start(bf16[1,96,96]{2,1,0:T(8,128)(2,1)} %param.36) | copy-start | bytes 55300
  133.0 28.5 %copy-start.13 = (bf16[1,96,96]{2,1,0:T(8,128)(2,1)S(1)}, bf16[1,96,96]{2,1,0:T(8,128)(2,1)}, u32[]{:S(2)}) copy-start(bf16[1,96,96]{2,1,0:T(8,128)(2,1)} %param.35) | copy-start | bytes 55300
  133.0 28.5 %copy-start.14 = (bf16[1,96,96]{2,1,0:T(8,128)(2,1)S(1)}, bf16[1,96,96]{2,1,0:T(8,128)(2,1)}, u32[]{:S(2)}) copy-start(bf16[1,96,96]{2,1,0:T(8,128)(2,1)} %param.34) | copy-start | bytes 55300
  180.6 13.3 %copy-start.6 = (s32[1,1,1536]{2,1,0:T(1,128)S(1)}, s32[1,1,1536]{2,1,0:T(1,128)}, u32[]{:S(2)}) copy-start(s32[1,1,1536]{2,1,0:T(1,128)} %param.31) | copy-start | bytes 18436
  186.8 40.3 %all-to-all-start.2 = ((bf16[96,128,12]{0,2,1:T(8,128)(2,1)}), bf16[96,128,12]{0,2,1:T(8,128)(2,1)S(1)}, u32[]{:S(2)}, u32[]{:S(2)}) async-start(bf16[96,128,12]{0,2,1:T(8,128)(2,1)} %reshape.419), calls=%async_computation.2 | async-start | bytes 1048576 | tf_op jit(solution)/shard_map/all_to_all | solution.py:203
where the time goes:
time: 235 us; the launch traced here: 233 us
  local copies, waits for them, and re-layouts  82.5 us (35%)
  waiting for transfers between devices  57.5 us (24%)
  starting transfers between devices  54.6 us (23%)
  matrix products  26 us (11%)
  other arithmetic  7.77 us (3%)
  between operations  4.41 us (2%)
    all_to_all x1, waiting for transfers between devices, shards(): lax.all_to_all(owner_slots, 'space', split_axis=1, concat_axis=1, tiled=T...  33.2 us
    all_to_all x1, waiting for transfers between devices, shards(): lax.all_to_all(outbound, 'space', split_axis=1, concat_axis=1, tiled=True)  23.2 us
    all_to_all x1, starting transfers between devices, shards(): lax.all_to_all(outbound_mask, 'space', split_axis=1, concat_axis=1, tiled...  17.3 us
    all_to_all x1, starting transfers between devices, shards(): lax.all_to_all(outbound, 'space', split_axis=1, concat_axis=1, tiled=True)  17 us
    concatenate x3, local copies, waits for them, and re-layouts, shards(): jnp.concatenate([padded[:, :, shift_x:shift_x + EDGE, shift_y:shift_y + E...  13.4 us
    ppermute x3, starting transfers between devices, shifted(): return lax.ppermute(block, axis, route)  13.2 us
    gather x2, local copies, waits for them, and re-layouts, shards(): jnp.take(block_table, gather_index.reshape(-1), axis=1)  9.62 us
    gather x1, local copies, waits for them, and re-layouts, shards(): jnp.take(active.astype(jnp.bfloat16), order_out)  9.46 us
  transfers between devices with their start and end apart: 6, of which 3 were waited for; matrix products, arithmetic and copies ran while one was open for 33% of the time, Pallas kernels for 0%

commit v1 on v0

v1 whole, which is shorter than its diff:
```python
import math

import jax
import jax.numpy as jnp
from jax import lax
from jax.experimental import pallas as pl
from jax.experimental.pallas import tpu as pltpu
from jax.sharding import PartitionSpec as P

HEADS = 6
HEAD_DIM = 16
EDGE = 8
PATCH = 384
EPSILON = 1e-05
MASK_FILL = -1e30
LANES = 128
VOX = EDGE**3
ROWS = 10


def shifted(block, axis, distance):
    devices = range(lax.axis_size(axis))
    route = [(i - distance, i) for i in devices if i - distance in devices]
    return lax.ppermute(block, axis, route)


def vmem():
    return pl.BlockSpec(memory_space=pltpu.VMEM)


def smem():
    return pl.BlockSpec(memory_space=pltpu.SMEM)


def lane_of(shape):
    return lax.broadcasted_iota(jnp.int32, shape, len(shape) - 1)


def copy_rows(count, read_index, write_index, src, dst):
    step = 16

    def body(outer, carry):
        base = outer * step
        for inner in range(step):
            i = base + inner
            dst[pl.ds(write_index(i), 1), :] = src[pl.ds(read_index(i), 1), :]
        return carry

    lax.fori_loop(0, count // step, body, 0)


def pack_rows(slots, packed, with_mask):
    peers = slots.shape[0] // 12
    lane = lane_of((peers, LANES))
    tokens = [slots[t * peers : (t + 1) * peers, :] for t in range(12)]
    for group in range(3):
        extra = tokens[4 * group + 3]
        for j in range(3):
            row = jnp.where(
                lane < 96, tokens[4 * group + j], pltpu.roll(extra, 96 - 32 * j, axis=1)
            )
            packed[pl.ds(3 * group + j, peers, stride=ROWS), :] = row
    last = jnp.zeros((peers, LANES), jnp.float32)
    if with_mask:
        for t in range(12):
            last = jnp.where(lane == t, pltpu.roll(tokens[t], 32 + t, axis=1), last)
    packed[pl.ds(ROWS - 1, peers, stride=ROWS), :] = last


def unpack_rows(packed, slots, with_mask):
    peers = slots.shape[0] // 12
    lane = lane_of((peers, LANES))
    if with_mask:
        flags = packed[pl.ds(ROWS - 1, peers, stride=ROWS), :]
    for group in range(3):
        rows = [packed[pl.ds(3 * group + j, peers, stride=ROWS), :] for j in range(3)]
        extra = jnp.zeros((peers, LANES), jnp.float32)
        for j in range(3):
            spot = (lane >= 32 * j) & (lane < 32 * j + 32)
            extra = jnp.where(spot, pltpu.roll(rows[j], (32 * j + 32) % LANES, axis=1), extra)
        for j in range(4):
            t = 4 * group + j
            value = rows[j] if j < 3 else extra
            value = jnp.where(lane < 96, value, 0.0)
            if with_mask:
                value = jnp.where(lane == 96, pltpu.roll(flags, 96 - t, axis=1), value)
            slots[t * peers : (t + 1) * peers, :] = value


def layout_kernel(feats, mask, table):
    tokens = feats.shape[1]
    flags = mask[...].astype(jnp.float32)
    values = feats[...].astype(jnp.float32) * flags
    row = lax.broadcasted_iota(jnp.int32, (LANES - 96, tokens), 0)
    tail = jnp.where(row == 0, jnp.broadcast_to(flags, row.shape), 0.0)
    table[...] = jnp.concatenate([values, tail], axis=0).T


def conv_kernel(rules, own, low, high, weights, joined, pooled, table, padded, views, halves):
    blocks = own.shape[0] // VOX
    pad_lanes = jnp.zeros((LANES - 96, VOX), jnp.float32)
    for b in range(blocks):
        table[b] = own[b * VOX : (b + 1) * VOX, :].reshape(EDGE, EDGE, EDGE, LANES)
    for spot, ref in ((blocks, low), (blocks + 1, high)):
        values = jnp.concatenate([ref[...].astype(jnp.float32), pad_lanes], axis=0).T
        table[spot] = values.reshape(EDGE, EDGE, EDGE, LANES)
    table[blocks + 2] = jnp.zeros((EDGE, EDGE, EDGE, LANES), jnp.float32)

    def span(direction):
        if direction < 0:
            return pl.ds(EDGE - 1, 1), pl.ds(0, 1)
        if direction > 0:
            return pl.ds(0, 1), pl.ds(EDGE + 1, 1)
        return pl.ds(0, EDGE), pl.ds(1, EDGE)

    for b in range(blocks):

        def neighbor(dx, dy, dz):
            k = 9 * (dx + 1) + 3 * (dy + 1) + dz + 1
            if k == 13:
                return b
            return rules[b, k if k < 13 else k - 1]

        for dx in (-1, 0, 1):
            sx, tx = span(dx)
            for dy in (-1, 0, 1):
                sy, ty = span(dy)
                here = table[neighbor(dx, dy, 0), sx, sy, :, :]
                below = table[neighbor(dx, dy, -1), sx, sy, :, :]
                above = table[neighbor(dx, dy, 1), sx, sy, :, :]
                z = lax.broadcasted_iota(jnp.int32, here.shape, 2)
                shape = here.shape
                flat = (shape[0] * shape[1] * EDGE, LANES)
                lower = jnp.where(z == EDGE - 1, below, here)
                upper = jnp.where(z == 0, above, here)
                padded[0, tx, ty, :, :] = pltpu.roll(lower, 1, axis=2)
                padded[1, tx, ty, :, :] = here
                padded[2, tx, ty, :, :] = pltpu.roll(upper, EDGE - 1, axis=2)
        for dy in range(3):
            for dz in range(3):
                k = dy * 3 + dz
                window = padded[dz, :, dy : dy + EDGE, :, :]
                views[:, k * LANES : (k + 1) * LANES] = window.reshape(
                    (EDGE + 2) * EDGE * EDGE, LANES
                ).astype(jnp.bfloat16)
        total = jnp.zeros((VOX, LANES), jnp.float32)
        for dx in range(3):
            total = total + jnp.dot(
                views[dx * 64 : dx * 64 + VOX, :], weights[dx], preferred_element_type=jnp.float32
            )
        rows = own[b * VOX : (b + 1) * VOX, :]
        conv = total * rows[:, 96:97]
        joined[b * VOX : (b + 1) * VOX, :] = rows + conv
        quads = conv.reshape(4, 2, 4, 2, EDGE, LANES)
        summed = (quads[:, 0, :, 0] + quads[:, 0, :, 1]) + (quads[:, 1, :, 0] + quads[:, 1, :, 1])
        halves[...] = summed.reshape(16 * EDGE, LANES)
        even = halves[pl.ds(0, 64, stride=2), :]
        odd = halves[pl.ds(1, 64, stride=2), :]
        pooled[b * 64 : (b + 1) * 64, :] = ((even + odd) * 0.125).astype(jnp.bfloat16)


def join_kernel(
    octants, order, joined, coarser, hidden, message, wide, children, rows, slots, packed
):
    blocks = joined.shape[0] // VOX
    wide[...] = coarser[...].astype(jnp.float32)
    count = blocks * 16
    for k in range(4):
        value = wide[pl.ds(k, count, stride=4), :]
        children[pl.ds(k, count, stride=8), :] = value
        children[pl.ds(k + 4, count, stride=8), :] = value
    children[count * 8 : count * 8 + 128, :] = jnp.zeros((128, LANES), jnp.float32)
    z = lax.broadcasted_iota(jnp.int32, (4, 4, EDGE, LANES), 2)
    lane = lax.broadcasted_iota(jnp.int32, (VOX, LANES), 1)
    for b in range(blocks):
        halves = []
        for ox in range(2):
            parts = []
            for oy in range(2):
                near = children[pl.ds(octants[b, 4 * ox + 2 * oy] * 128, 128), :]
                far = children[pl.ds(octants[b, 4 * ox + 2 * oy + 1] * 128, 128), :]
                near = near.reshape(4, 4, EDGE, LANES)
                far = far.reshape(4, 4, EDGE, LANES)
                parts.append(jnp.where(z < 4, near, far))
            halves.append(jnp.concatenate(parts, axis=1))
        lifted = jnp.concatenate(halves, axis=0).reshape(VOX, LANES)
        here = joined[b * VOX : (b + 1) * VOX, :]
        flags = here[:, 96:97]
        value = jnp.where(lane < 96, (here + lifted) * flags, here)
        short = value.astype(jnp.bfloat16)
        hidden[b * VOX : (b + 1) * VOX, :] = short
        rows[b * VOX : (b + 1) * VOX, :] = short.astype(jnp.float32)
    copy_rows(rows.shape[0], lambda i: order[i], lambda i: i, rows, slots)
    pack_rows(slots, packed, True)
    message[...] = packed[...].astype(jnp.bfloat16)


def attend_kernel(
    order, inbound, gain, w_query, w_key, w_value, outbound,
    packed, slots, rows, scores, keys, attended,
):
    packed[...] = inbound[...].astype(jnp.float32)
    unpack_rows(packed, slots, True)
    copy_rows(rows.shape[0], lambda i: order[i], lambda i: i, slots, rows)
    lane = lane_of((PATCH, LANES))
    inside = lane < 96
    row = lax.broadcasted_iota(jnp.int32, (PATCH, PATCH), 0)
    own = row == lax.broadcasted_iota(jnp.int32, (PATCH, PATCH), 1)
    contract = (((1,), (1,)), ((), ()))
    for patch in range(rows.shape[0] // PATCH):
        serial = rows[patch * PATCH : (patch + 1) * PATCH, :]
        flags = serial[:, 96:97]
        values = jnp.where(inside, serial, 0.0)
        center = jnp.sum(values, axis=1, keepdims=True) * (1.0 / 96)
        spread = jnp.where(inside, values - center, 0.0)
        variance = jnp.sum(spread * spread, axis=1, keepdims=True) * (1.0 / 96)
        normed = (spread * lax.rsqrt(variance + EPSILON) * gain[...]).astype(jnp.bfloat16)
        query = lax.dot_general(w_query[...], normed, contract, preferred_element_type=jnp.float32)
        query = (query * (1.0 / math.sqrt(HEAD_DIM))).astype(jnp.bfloat16)
        keyed = lax.dot_general(normed, w_key[...], contract, preferred_element_type=jnp.float32)
        valued = lax.dot_general(w_value[...], normed, contract, preferred_element_type=jnp.float32)
        valued = valued.astype(jnp.bfloat16)
        for head in range(HEADS):
            spot = (lane >= head * HEAD_DIM) & (lane < (head + 1) * HEAD_DIM)
            keys[head * PATCH : (head + 1) * PATCH, :] = jnp.where(spot, keyed, 0.0).astype(
                jnp.bfloat16
            )
        scores[...] = jnp.dot(keys[...], query, preferred_element_type=jnp.float32)
        bias = jnp.where((flags > 0) | own, 0.0, MASK_FILL)
        ones = jnp.ones((HEAD_DIM, PATCH), jnp.bfloat16)
        for head in range(HEADS):
            here = scores[head * PATCH : (head + 1) * PATCH, :] + bias
            top = jnp.max(here, axis=0, keepdims=True)
            exponent = jnp.exp(here - top).astype(jnp.bfloat16)
            left = jnp.concatenate(
                [valued[head * HEAD_DIM : (head + 1) * HEAD_DIM, :], ones], axis=0
            )
            mixed = jnp.dot(left, exponent, preferred_element_type=jnp.float32)
            attended[head * HEAD_DIM : (head + 1) * HEAD_DIM, :] = (
                mixed[:HEAD_DIM] / mixed[HEAD_DIM : HEAD_DIM + 1]
            )
        rows[patch * PATCH : (patch + 1) * PATCH, :] = attended[...].T
    copy_rows(rows.shape[0], lambda i: i, lambda i: order[i], rows, slots)
    pack_rows(slots, packed, False)
    outbound[...] = packed[...].astype(jnp.bfloat16)


def finish_kernel(order, returned, hidden, mask, w_out, result, packed, slots, rows):
    packed[...] = returned[...].astype(jnp.float32)
    unpack_rows(packed, slots, False)
    copy_rows(rows.shape[0], lambda i: i, lambda i: order[i], slots, rows)
    projected = lax.dot_general(
        w_out[...],
        rows[...].astype(jnp.bfloat16),
        (((1,), (1,)), ((), ())),
        preferred_element_type=jnp.float32,
    )
    value = hidden[...].astype(jnp.float32) + projected
    result[...] = (value * mask[...].astype(jnp.float32)).astype(jnp.bfloat16)


def exchange(packed):
    spaces = lax.axis_size("space")
    tiles = packed.reshape(packed.shape[0] // 2, 2, LANES)
    return lax.all_to_all(tiles, "space", split_axis=0, concat_axis=0, tiled=True).reshape(
        packed.shape
    )


def shards(
    feats,
    mask,
    conv_w,
    rules,
    send_lists,
    pool_map,
    send_order,
    patch_order,
    ln_gain,
    w_query,
    w_key,
    w_value,
    w_out,
):
    f32, bf16 = jnp.float32, jnp.bfloat16
    tokens = feats.shape[2]
    blocks = tokens // VOX
    spaces = lax.axis_size("space")
    pair = tokens // spaces
    packed_rows = spaces * ROWS

    def boundary(row_index):
        start = send_lists[0, 0, row_index, 0] * VOX
        piece = lax.dynamic_slice(feats[0], (0, start), (96, VOX))
        flags = lax.dynamic_slice(mask, (0, start), (1, VOX))
        return piece * flags.astype(bf16)

    low = shifted(boundary(1), "space", 1)
    high = shifted(boundary(0), "space", -1)
    table = pl.pallas_call(
        layout_kernel,
        out_shape=jax.ShapeDtypeStruct((tokens, LANES), f32),
        in_specs=[vmem()] * 2,
        out_specs=vmem(),
        name="layout",
    )(feats[0], mask)
    weights = jnp.pad(conv_w[0].transpose(0, 2, 1), ((0, 0), (0, LANES - 96), (0, LANES - 96)))
    weights = weights.reshape(3, 9 * LANES, LANES)
    joined, pooled = pl.pallas_call(
        conv_kernel,
        out_shape=(
            jax.ShapeDtypeStruct((tokens, LANES), f32),
            jax.ShapeDtypeStruct((blocks * 64, LANES), bf16),
        ),
        in_specs=[smem()] + [vmem()] * 4,
        out_specs=(vmem(), vmem()),
        scratch_shapes=[
            pltpu.VMEM((blocks + 3, EDGE, EDGE, EDGE, LANES), f32),
            pltpu.VMEM((3, EDGE + 2, EDGE + 2, EDGE, LANES), f32),
            pltpu.VMEM(((EDGE + 2) * EDGE * EDGE, 9 * LANES), bf16),
            pltpu.VMEM((16 * EDGE, LANES), f32),
        ],
        name="conv",
    )(rules[0], table, low, high, weights)
    coarser = shifted(pooled, "section", 1)
    order_out = send_order[0, 0].reshape(spaces, pair).T.reshape(-1)
    held = patch_order[0, 0]
    order_in = (held % pair) * spaces + held // pair
    hidden, message = pl.pallas_call(
        join_kernel,
        out_shape=(
            jax.ShapeDtypeStruct((tokens, LANES), bf16),
            jax.ShapeDtypeStruct((packed_rows, LANES), bf16),
        ),
        in_specs=[smem()] * 2 + [vmem()] * 2,
        out_specs=(vmem(), vmem()),
        scratch_shapes=[
            pltpu.VMEM((blocks * 64, LANES), f32),
            pltpu.VMEM(((blocks + 1) * 128, LANES), f32),
            pltpu.VMEM((tokens, LANES), f32),
            pltpu.VMEM((tokens, LANES), f32),
            pltpu.VMEM((packed_rows, LANES), f32),
        ],
        name="join",
    )(pool_map[0], order_out, joined, coarser)
    inbound = exchange(message)

    def square(weight):
        return jnp.pad(weight[0], ((0, LANES - 96), (0, LANES - 96)))

    outbound = pl.pallas_call(
        attend_kernel,
        out_shape=jax.ShapeDtypeStruct((packed_rows, LANES), bf16),
        in_specs=[smem()] + [vmem()] * 5,
        out_specs=vmem(),
        scratch_shapes=[
            pltpu.VMEM((packed_rows, LANES), f32),
            pltpu.VMEM((tokens, LANES), f32),
            pltpu.VMEM((tokens, LANES), f32),
            pltpu.VMEM((HEADS * PATCH, PATCH), f32),
            pltpu.VMEM((HEADS * PATCH, LANES), bf16),
            pltpu.VMEM((LANES, PATCH), f32),
        ],
        name="attend",
    )(
        order_in,
        inbound,
        jnp.pad(ln_gain.astype(f32), ((0, 0), (0, LANES - 96))),
        square(w_query),
        square(w_key),
        square(w_value),
    )
    returned = exchange(outbound)
    result = pl.pallas_call(
        finish_kernel,
        out_shape=jax.ShapeDtypeStruct((96, tokens), bf16),
        in_specs=[smem()] + [vmem()] * 4,
        out_specs=vmem(),
        scratch_shapes=[
            pltpu.VMEM((packed_rows, LANES), f32),
            pltpu.VMEM((tokens, LANES), f32),
            pltpu.VMEM((tokens, LANES), f32),
        ],
        name="finish",
    )(
        order_out,
        returned,
        hidden[:, :96].T,
        mask,
        jnp.pad(w_out[0], ((0, 0), (0, LANES - 96))),
    )
    return result[None]


def solution(mesh):
    placed = (
        P("section", None, "space"),
        P("section", "space"),
        P("section", None, None, None),
        P("section", "space", None),
        P("section", "space", None, None),
        P("section", "space", None),
        P("section", "space", None),
        P("section", "space", None),
        P("section", None),
        P("section", None, None),
        P("section", None, None),
        P("section", None, None),
        P("section", None, None),
    )
    return jax.shard_map(
        shards, mesh=mesh, in_specs=placed, out_specs=P("section", None, "space"), check_vma=False
    )
```

time: 235 us -> 130 us (0.55)
  local copies, waits for them, and re-layouts: 82.5 us -> 12.3 us
  Pallas kernels: 0 us -> 27.7 us
  matrix products: 26 us -> 0 us
  starting transfers between devices: 54.6 us -> 38.6 us
  waiting for transfers between devices: 57.5 us -> 46 us
  other arithmetic: 7.77 us -> 2.28 us
  between operations: 4.41 us -> 1.46 us
    gather x10 -> x0, local copies, waits for them, and re-layouts: 42.3 us -> none  [the longest x2 9.62 us: shards(): jnp.take(block_table, gather_index.reshape(-1), axis=1)]
    pallas_call x0 -> x5, Pallas kernels: none -> 27.7 us  [the longest x1 11.4 us: shards(): pl.pallas_call(attend_kernel, out_shape=jax.ShapeDtypeStruct((packed_rows...]
    dot_general x7 -> x0, matrix products: 17 us -> none  [the longest x2 7.32 us: one_group(): jnp.einsum('phqk,phdk->phdq', weights, pieces[2], preferred_element_type=...]
    concatenate x7 -> x0, local copies, waits for them, and re-layouts: 14.3 us -> none  [the longest x3 13.4 us: shards(): jnp.concatenate([padded[:, :, shift_x:shift_x + EDGE, shift_y:shift_y + E...]
    all_to_all x3 -> x2, starting transfers between devices: 41.5 us -> 27.3 us  [exchange(): lax.all_to_all(tiles, 'space', split_axis=0, concat_axis=0, tiled=True)]
    all_to_all x3 -> x2, waiting for transfers between devices: 56.4 us -> 45.9 us  [exchange(): lax.all_to_all(tiles, 'space', split_axis=0, concat_axis=0, tiled=True)]
    scatter x2 -> x0, local copies, waits for them, and re-layouts: 9.1 us -> none  [the longest x1 4.55 us: shards(): jnp.zeros_like(attended).at[:, order_in].set(attended)]
    sub x2 -> x0, matrix products: 9 us -> none  [one_group(): exponent = jnp.exp(scores - row_max)]
  transfers between devices with their start and end apart: 6 -> 5, of which waited for: 3 -> 3; matrix products, arithmetic and copies ran while one was open for 33% -> 7% of each run, Pallas kernels for 0% -> 2%
where the time goes in v1:
time: 130 us; the launch traced here: 128 us
  waiting for transfers between devices  46 us (35%)
  starting transfers between devices  38.6 us (30%)
  Pallas kernels  27.7 us (21%)
  local copies, waits for them, and re-layouts  12.3 us (9%)
  other arithmetic  2.28 us (2%)
  between operations  1.46 us (1%)
    all_to_all x2, waiting for transfers between devices, exchange(): lax.all_to_all(tiles, 'space', split_axis=0, concat_axis=0, tiled=True)  45.9 us
    all_to_all x2, starting transfers between devices, exchange(): lax.all_to_all(tiles, 'space', split_axis=0, concat_axis=0, tiled=True)  27.3 us
    pallas_call x1, Pallas kernels, shards(): pl.pallas_call(attend_kernel, out_shape=jax.ShapeDtypeStruct((packed_rows...  11.4 us
    ppermute x3, starting transfers between devices, shifted(): return lax.ppermute(block, axis, route)  11.3 us
    pallas_call x1, Pallas kernels, shards(): pl.pallas_call(conv_kernel, out_shape=(jax.ShapeDtypeStruct((tokens, LANE...  5.96 us
    unnamed x35, local copies, waits for them, and re-layouts  5.62 us
    pallas_call x1, Pallas kernels, shards(): pl.pallas_call(join_kernel, out_shape=(jax.ShapeDtypeStruct((tokens, LANE...  4.27 us
    pallas_call x1, Pallas kernels, shards(): pl.pallas_call(finish_kernel, out_shape=jax.ShapeDtypeStruct((96, tokens)...  3.93 us
  transfers between devices with their start and end apart: 5, of which 3 were waited for; matrix products, arithmetic and copies ran while one was open for 7% of the time, Pallas kernels for 2%

profile of v1, /device:TPU:1, one launch (start us, length us, event | category | flops | bytes accessed | tf_op | source)
XLA Modules:
  0.0 128.3 jit_solution(15177758676953690083)
XLA Ops:
  0.0 1.4 %fusion.2 = (s32[1,1,1,1]{2,3,1,0:T(1,128)}, s32[1,1,1,1]{2,3,1,0:T(1,128)}) fusion(s32[1,1,2,1]{2,3,1,0:T(1,128)} %param.17), kind=kLoop, calls=%fused_computation.15 | loop fusion | bytes 16 | tf_op jit(solution)/shard_map/slice | solution.py:293
  2.7 1.0 bitcast_multiply_fusion
  3.7 4.9 %collective-permute-start = (bf16[96,512]{1,0:T(8,128)(2,1)S(1)}, bf16[96,512]{1,0:T(8,128)(2,1)S(1)}, u32[]{:S(2)}, u32[]{:S(2)}) collective-permute-start(bf16[96,512]{1,0:T(8,128)(2,1)S(1)} %get-tuple-element.18), channel_id=1, source_target_pairs={{0,1},{1,2},{2,3},{3,4},{4,5},{5,6},{6,7},{7,8},{8,9},{9,10},{10,1... | collective-permute-start | bytes 294920 | tf_op jit(solution)/shard_map/ppermute | solution.py:24
  8.7 5.1 %collective-permute-start.1 = (bf16[96,512]{1,0:T(8,128)(2,1)S(1)}, bf16[96,512]{1,0:T(8,128)(2,1)S(1)}, u32[]{:S(2)}, u32[]{:S(2)}) collective-permute-start(bf16[96,512]{1,0:T(8,128)(2,1)S(1)} %get-tuple-element.17), channel_id=1, source_target_pairs={{1,0},{2,1},{3,2},{4,3},{5,4},{6,5},{7,6},{8,7},{9,8},{10,9},{11,1... | collective-permute-start | bytes 294920 | tf_op jit(solution)/shard_map/ppermute | solution.py:24
  13.8 1.4 %copy.21 = bf16[27,96,96]{2,1,0:T(8,128)(2,1)S(1)} copy(bf16[27,96,96]{1,2,0:T(8,128)(2,1)} %bitcast.35) | data formatting | bytes 995328
  15.2 2.1 %layout.1.own = f32[1536,128]{1,0:T(8,128)} custom-call(bf16[96,1536]{1,0:T(8,128)(2,1)} %bitcast.34, s32[1,1536]{1,0:T(1,128)} %mask.3), custom_call_target="tpu_custom_call" | custom-call | tf_op jit(solution)/shard_map/layout/pallas_call | solution.py:300
  17.9 1.2 pad.24.clone
  19.1 0.6 copy-done.3
  19.7 6.0 %conv.1 = (f32[1536,128]{1,0:T(8,128)}, bf16[192,128]{1,0:T(8,128)(2,1)}) custom-call(s32[3,26]{1,0:T(4,128)} %bitcast.45, f32[1536,128]{1,0:T(8,128)} %layout.1.own, bf16[96,512]{1,0:T(8,128)(2,1)} %copy-done.3, bf16[96,512]{1,0:T(8,128)(2,1)} %copy-done.4, bf16[3,1152,128]{2,1,0:T(8,128)(2,1)} %bitcast.30), custom_call_target="tpu_custom_call" | custom-call | tf_op jit(solution)/shard_map/conv/pallas_call | solution.py:309
  25.7 1.3 collective-permute-start.2
  27.1 0.7 copy.16
  28.5 0.6 copy-done.5
  29.1 4.3 %join.1 = (bf16[1536,128]{1,0:T(8,128)(2,1)}, bf16[1280,128]{1,0:T(8,128)(2,1)}) custom-call(s32[3,8]{1,0:T(4,128)} %bitcast.44, s32[1536]{0:T(1024)} %bitcast.38, f32[1536,128]{1,0:T(8,128)} %get-tuple-element.9.joined, bf16[192,128]{1,0:T(8,128)(2,1)} %copy-done.5), custom_call_target="tpu_custom_call" | custom-call | tf_op jit(solution)/shard_map/join/pallas_call | solution.py:329
  33.4 20.1 %all-to-all-start = ((bf16[640,2,128]{2,1,0:T(2,128)(2,1)}), bf16[640,2,128]{2,1,0:T(2,128)(2,1)S(1)}, u32[]{:S(2)}, u32[]{:S(2)}) async-start(bf16[640,2,128]{2,1,0:T(2,128)(2,1)} %bitcast.36), calls=%async_computation | async-start | bytes 655360 | tf_op jit(solution)/shard_map/all_to_all | solution.py:265
  53.5 0.6 pad.27.w_query
  55.0 0.6 pad.29.w_value
  56.9 22.0 %all-to-all-done = bf16[640,2,128]{2,1,0:T(2,128)(2,1)S(1)} async-done(((bf16[640,2,128]{2,1,0:T(2,128)(2,1)}), bf16[640,2,128]{2,1,0:T(2,128)(2,1)S(1)}, u32[]{:S(2)}, u32[]{:S(2)}) %all-to-all-start) | async-done | bytes 327712 | tf_op jit(solution)/shard_map/all_to_all | solution.py:265
  78.9 0.7 copy-done
  79.6 11.4 %attend.1 = bf16[1280,128]{1,0:T(8,128)(2,1)} custom-call(s32[1536]{0:T(1024)} %fusion.1.order, bf16[1280,128]{1,0:T(8,128)(2,1)} %bitcast.31, f32[1,128]{1,0:T(1,128)} %pad_convert_fusion.gain, bf16[128,128]{1,0:T(8,128)(2,1)} %pad.27.w_query, bf16[128,128]{1,0:T(8,128)(2,1)} %pad.28.w_key, bf16[128,128]{1,0:T(8,128)(2,1)} %pad.29.w_value), custom_call_target="tpu_custom_call" | custom-call | tf_op jit(solution)/shard_map/attend/pallas_call | solution.py:351
  91.0 7.1 %all-to-all-start.1 = ((bf16[640,2,128]{2,1,0:T(2,128)(2,1)}), bf16[640,2,128]{2,1,0:T(2,128)(2,1)S(1)}, u32[]{:S(2)}, u32[]{:S(2)}) async-start(bf16[640,2,128]{2,1,0:T(2,128)(2,1)} %bitcast.32), calls=%async_computation.1 | async-start | bytes 655360 | tf_op jit(solution)/shard_map/all_to_all | solution.py:265
  98.9 0.7 slice_bitcast_fusion.hidden
  99.7 23.9 %all-to-all-done.1 = bf16[640,2,128]{2,1,0:T(2,128)(2,1)S(1)} async-done(((bf16[640,2,128]{2,1,0:T(2,128)(2,1)}), bf16[640,2,128]{2,1,0:T(2,128)(2,1)S(1)}, u32[]{:S(2)}, u32[]{:S(2)}) %all-to-all-start.1) | async-done | bytes 327712 | tf_op jit(solution)/shard_map/all_to_all | solution.py:265
  123.6 0.7 copy-done.1
  124.3 3.9 %finish.1 = bf16[96,1536]{1,0:T(8,128)(2,1)} custom-call(s32[1536]{0:T(1024)} %bitcast.39, bf16[1280,128]{1,0:T(8,128)(2,1)} %bitcast.33, bf16[96,1536]{1,0:T(8,128)(2,1)} %slice_bitcast_fusion.hidden, s32[1,1536]{1,0:T(1,128)} %mask.3, bf16[96,128]{1,0:T(8,128)(2,1)} %pad.30.w_out), custom_call_target="tpu_custom_call" | custom-call | tf_op jit(solution)/shard_map/finish/pallas_call | solution.py:374
  (43 shorter events, 4.4 us)
Async XLA Ops:
  2.0 0.7 copy-start.6
  3.7 15.3 %collective-permute-start = (bf16[96,512]{1,0:T(8,128)(2,1)S(1)}, bf16[96,512]{1,0:T(8,128)(2,1)S(1)}, u32[]{:S(2)}, u32[]{:S(2)}) collective-permute-start(bf16[96,512]{1,0:T(8,128)(2,1)S(1)} %get-tuple-element.18), channel_id=1, source_target_pairs={{0,1},{1,2},{2,3},{3,4},{4,5},{5,6},{6,7},{7,8},{8,9},{9,10},{10,1... | collective-permute-start | bytes 294920 | tf_op jit(solution)/shard_map/ppermute | solution.py:24
  8.7 10.4 %collective-permute-start.1 = (bf16[96,512]{1,0:T(8,128)(2,1)S(1)}, bf16[96,512]{1,0:T(8,128)(2,1)S(1)}, u32[]{:S(2)}, u32[]{:S(2)}) collective-permute-start(bf16[96,512]{1,0:T(8,128)(2,1)S(1)} %get-tuple-element.17), channel_id=1, source_target_pairs={{1,0},{2,1},{3,2},{4,3},{5,4},{6,5},{7,6},{8,7},{9,8},{10,9},{11,1... | collective-permute-start | bytes 294920 | tf_op jit(solution)/shard_map/ppermute | solution.py:24
  15.2 2.1 %copy-start.13 = (s32[1,3,26]{2,0,1:T(1,128)S(1)}, s32[1,3,26]{2,0,1:T(1,128)}, u32[]{:S(2)}) copy-start(s32[1,3,26]{2,0,1:T(1,128)} %param.16) | copy-start | bytes 940
  19.1 0.6 copy-start.3
  19.1 0.7 copy-start.4
  19.7 7.2 %copy-start.12 = (s32[1,1,1536]{2,1,0:T(1,128)S(1)}, s32[1,1,1536]{2,1,0:T(1,128)}, u32[]{:S(2)}) copy-start(s32[1,1,1536]{2,1,0:T(1,128)} %param.19) | copy-start | bytes 18436
  25.7 2.8 %collective-permute-start.2 = (bf16[192,128]{1,0:T(8,128)(2,1)}, bf16[192,128]{1,0:T(8,128)(2,1)S(1)}, u32[]{:S(2)}, u32[]{:S(2)}) collective-permute-start(bf16[192,128]{1,0:T(8,128)(2,1)} %get-tuple-element.10), channel_id=1, source_target_pairs={{0,128},{128,256},{256,384},{1,129},{129,257},{257,385},{2,130},{1... | collective-permute-start | bytes 147464 | tf_op jit(solution)/shard_map/ppermute | solution.py:24
  27.1 0.7 copy-start.14
  28.5 0.6 copy-start.5
  33.4 20.1 %copy-start.7 = (bf16[1,96,96]{2,1,0:T(8,128)(2,1)S(1)}, bf16[1,96,96]{2,1,0:T(8,128)(2,1)}, u32[]{:S(2)}) copy-start(bf16[1,96,96]{2,1,0:T(8,128)(2,1)} %param.22) | copy-start | bytes 55300
  33.4 45.5 %all-to-all-start = ((bf16[640,2,128]{2,1,0:T(2,128)(2,1)}), bf16[640,2,128]{2,1,0:T(2,128)(2,1)S(1)}, u32[]{:S(2)}, u32[]{:S(2)}) async-start(bf16[640,2,128]{2,1,0:T(2,128)(2,1)} %bitcast.36), calls=%async_computation | async-start | bytes 655360 | tf_op jit(solution)/shard_map/all_to_all | solution.py:265
  53.5 0.7 copy-start.8
  54.2 0.7 copy-start.9
  54.2 1.9 %copy-start.11 = (s32[1,1,1536]{2,1,0:T(1,128)S(1)}, s32[1,1,1536]{2,1,0:T(1,128)}, u32[]{:S(2)}) copy-start(s32[1,1,1536]{2,1,0:T(1,128)} %param.20) | copy-start | bytes 18436
  55.0 0.7 copy-start.15
  78.9 0.7 copy-start
  91.0 7.8 %copy-start.2 = (bf16[1536,128]{1,0:T(8,128)(2,1)S(1)}, bf16[1536,128]{1,0:T(8,128)(2,1)}, u32[]{:S(2)}) copy-start(bf16[1536,128]{1,0:T(8,128)(2,1)} %get-tuple-element.12) | copy-start | bytes 1179652
  91.0 7.1 %copy-start.10 = (bf16[1,96,96]{2,1,0:T(8,128)(2,1)S(1)}, bf16[1,96,96]{2,1,0:T(8,128)(2,1)}, u32[]{:S(2)}) copy-start(bf16[1,96,96]{2,1,0:T(8,128)(2,1)} %param.25) | copy-start | bytes 55300
  91.0 32.6 %all-to-all-start.1 = ((bf16[640,2,128]{2,1,0:T(2,128)(2,1)}), bf16[640,2,128]{2,1,0:T(2,128)(2,1)S(1)}, u32[]{:S(2)}, u32[]{:S(2)}) async-start(bf16[640,2,128]{2,1,0:T(2,128)(2,1)} %bitcast.32), calls=%async_computation.1 | async-start | bytes 655360 | tf_op jit(solution)/shard_map/all_to_all | solution.py:265
  123.6 0.7 copy-start.1

commit v2 on v1

--- a/solution.py
+++ b/solution.py
@@ -16,6 +16,8 @@
 LANES = 128
 VOX = EDGE**3
 ROWS = 10
+CONTRACT_LAST = (((1,), (1,)), ((), ()))
+VMEM_LIMIT = 24 << 20
 
 
 def shifted(block, axis, distance):
@@ -87,13 +89,32 @@
             slots[t * peers : (t + 1) * peers, :] = value
 
 
-def layout_kernel(feats, mask, table):
+def send_kernel(lists, feats, mask, to_upper, to_lower):
+    for out, row_index in ((to_upper, 1), (to_lower, 0)):
+        here = pl.ds(pl.multiple_of(lists[row_index] * VOX, VOX), VOX)
+        flags = mask[:, here].astype(jnp.float32)
+        out[...] = (feats[:, here].astype(jnp.float32) * flags).astype(jnp.bfloat16)
+
+
+def layout_kernel(octants, feats, mask, taps, table, weights):
     tokens = feats.shape[1]
     flags = mask[...].astype(jnp.float32)
     values = feats[...].astype(jnp.float32) * flags
+    token = lax.broadcasted_iota(jnp.int32, (1, tokens), 1)
+    x, y, z = (token >> 6) & 7, (token >> 3) & 7, token & 7
+    octant = ((token >> 9) << 3) + ((x >> 2) << 2) + ((y >> 2) << 1) + (z >> 2)
+    slot = jnp.full((1, tokens), 3, jnp.int32)
+    for k in range(octants.shape[0]):
+        slot = jnp.where(octant == k, octants[k], slot)
+    within = ((x & 3) << 4) + ((y & 3) << 2) + (z & 3)
+    child = jnp.where((slot < 3) & (mask[...] > 0), slot * 64 + within, 255).astype(jnp.float32)
     row = lax.broadcasted_iota(jnp.int32, (LANES - 96, tokens), 0)
-    tail = jnp.where(row == 0, jnp.broadcast_to(flags, row.shape), 0.0)
+    tail = jnp.where(row == 0, flags, jnp.where(row == 1, child, 0.0))
     table[...] = jnp.concatenate([values, tail], axis=0).T
+    weights[...] = jnp.zeros(weights.shape, jnp.bfloat16)
+    for k in range(27):
+        at = (k % 9) * LANES
+        weights[k // 9, 0:96, at : at + 96] = taps[k]
 
 
 def conv_kernel(rules, own, low, high, weights, joined, pooled, table, padded, views, halves):
@@ -145,8 +166,11 @@
                 ).astype(jnp.bfloat16)
         total = jnp.zeros((VOX, LANES), jnp.float32)
         for dx in range(3):
-            total = total + jnp.dot(
-                views[dx * 64 : dx * 64 + VOX, :], weights[dx], preferred_element_type=jnp.float32
+            total = total + lax.dot_general(
+                views[dx * 64 : dx * 64 + VOX, :],
+                weights[dx],
+                CONTRACT_LAST,
+                preferred_element_type=jnp.float32,
             )
         rows = own[b * VOX : (b + 1) * VOX, :]
         conv = total * rows[:, 96:97]
@@ -159,55 +183,55 @@
         pooled[b * 64 : (b + 1) * 64, :] = ((even + odd) * 0.125).astype(jnp.bfloat16)
 
 
-def join_kernel(
-    octants, order, joined, coarser, hidden, message, wide, children, rows, slots, packed
-):
+def child_matrix(rows):
+    count = rows.shape[0]
+    column = lax.broadcasted_iota(jnp.int32, (count, 2 * LANES), 1).astype(jnp.float32)
+    return jnp.where(column == rows[:, 97:98], 1.0, 0.0).astype(jnp.bfloat16)
+
+
+def lift(rows, chosen, coarser):
+    blank = jnp.zeros((2 * LANES - coarser.shape[0], LANES), jnp.bfloat16)
+    below = jnp.concatenate([coarser, blank], axis=0)
+    return rows + jnp.dot(chosen, below, preferred_element_type=jnp.float32)
+
+
+def gather_kernel(order, joined, slots, chosen):
+    copy_rows(slots.shape[0], lambda i: order[i], lambda i: i, joined, slots)
+    chosen[...] = child_matrix(slots[...])
+
+
+def join_kernel(slots, chosen, coarser, message, lifted, packed):
+    lifted[...] = lift(slots[...], chosen[...], coarser[...])
+    pack_rows(lifted, packed, True)
+    message[...] = packed[...].astype(jnp.bfloat16)
+
+
+def residual_kernel(joined, coarser, hidden):
     blocks = joined.shape[0] // VOX
-    wide[...] = coarser[...].astype(jnp.float32)
-    count = blocks * 16
-    for k in range(4):
-        value = wide[pl.ds(k, count, stride=4), :]
-        children[pl.ds(k, count, stride=8), :] = value
-        children[pl.ds(k + 4, count, stride=8), :] = value
-    children[count * 8 : count * 8 + 128, :] = jnp.zeros((128, LANES), jnp.float32)
-    z = lax.broadcasted_iota(jnp.int32, (4, 4, EDGE, LANES), 2)
-    lane = lax.broadcasted_iota(jnp.int32, (VOX, LANES), 1)
     for b in range(blocks):
-        halves = []
-        for ox in range(2):
-            parts = []
-            for oy in range(2):
-                near = children[pl.ds(octants[b, 4 * ox + 2 * oy] * 128, 128), :]
-                far = children[pl.ds(octants[b, 4 * ox + 2 * oy + 1] * 128, 128), :]
-                near = near.reshape(4, 4, EDGE, LANES)
-                far = far.reshape(4, 4, EDGE, LANES)
-                parts.append(jnp.where(z < 4, near, far))
-            halves.append(jnp.concatenate(parts, axis=1))
-        lifted = jnp.concatenate(halves, axis=0).reshape(VOX, LANES)
-        here = joined[b * VOX : (b + 1) * VOX, :]
-        flags = here[:, 96:97]
-        value = jnp.where(lane < 96, (here + lifted) * flags, here)
-        short = value.astype(jnp.bfloat16)
-        hidden[b * VOX : (b + 1) * VOX, :] = short
-        rows[b * VOX : (b + 1) * VOX, :] = short.astype(jnp.float32)
-    copy_rows(rows.shape[0], lambda i: order[i], lambda i: i, rows, slots)
-    pack_rows(slots, packed, True)
-    message[...] = packed[...].astype(jnp.bfloat16)
+        rows = joined[b * VOX : (b + 1) * VOX, :]
+        value = lift(rows, child_matrix(rows), coarser[...])
+        hidden[:, b * VOX : (b + 1) * VOX] = value.T[:96].astype(jnp.bfloat16)
 
 
 def attend_kernel(
     order, inbound, gain, w_query, w_key, w_value, outbound,
-    packed, slots, rows, scores, keys, attended,
+    packed, slots, rows, keys, scores, exponents, diagonal, attended,
 ):
     packed[...] = inbound[...].astype(jnp.float32)
     unpack_rows(packed, slots, True)
     copy_rows(rows.shape[0], lambda i: order[i], lambda i: i, slots, rows)
-    lane = lane_of((PATCH, LANES))
+    lane = lane_of((1, LANES))
     inside = lane < 96
-    row = lax.broadcasted_iota(jnp.int32, (PATCH, PATCH), 0)
-    own = row == lax.broadcasted_iota(jnp.int32, (PATCH, PATCH), 1)
-    contract = (((1,), (1,)), ((), ()))
+    channel = lax.broadcasted_iota(jnp.int32, (LANES, PATCH), 0)
+    factor = math.log2(math.e) / math.sqrt(HEAD_DIM)
+    ones = jnp.ones((HEAD_DIM, PATCH), jnp.bfloat16)
+
+    def project(left, right):
+        return lax.dot_general(left, right, CONTRACT_LAST, preferred_element_type=jnp.float32)
+
     for patch in range(rows.shape[0] // PATCH):
+        side = patch % 2
         serial = rows[patch * PATCH : (patch + 1) * PATCH, :]
         flags = serial[:, 96:97]
         values = jnp.where(inside, serial, 0.0)
@@ -215,31 +239,38 @@
         spread = jnp.where(inside, values - center, 0.0)
         variance = jnp.sum(spread * spread, axis=1, keepdims=True) * (1.0 / 96)
         normed = (spread * lax.rsqrt(variance + EPSILON) * gain[...]).astype(jnp.bfloat16)
-        query = lax.dot_general(w_query[...], normed, contract, preferred_element_type=jnp.float32)
-        query = (query * (1.0 / math.sqrt(HEAD_DIM))).astype(jnp.bfloat16)
-        keyed = lax.dot_general(normed, w_key[...], contract, preferred_element_type=jnp.float32)
-        valued = lax.dot_general(w_value[...], normed, contract, preferred_element_type=jnp.float32)
-        valued = valued.astype(jnp.bfloat16)
+        query = project(w_query[...], normed) * factor
+        query = jnp.where(channel == 96, 1.0, query).astype(jnp.bfloat16)
+        keyed = project(normed, w_key[...])
+        keyed = jnp.where(lane == 96, jnp.where(flags > 0, 0.0, MASK_FILL), keyed)
+        keyed = keyed.astype(jnp.bfloat16)
+        keyed_across = project(w_key[...], normed).astype(jnp.bfloat16)
+        valued = project(w_value[...], normed).astype(jnp.bfloat16)
+        products = query.astype(jnp.float32) * keyed_across.astype(jnp.float32)
         for head in range(HEADS):
-            spot = (lane >= head * HEAD_DIM) & (lane < (head + 1) * HEAD_DIM)
-            keys[head * PATCH : (head + 1) * PATCH, :] = jnp.where(spot, keyed, 0.0).astype(
-                jnp.bfloat16
-            )
-        scores[...] = jnp.dot(keys[...], query, preferred_element_type=jnp.float32)
-        bias = jnp.where((flags > 0) | own, 0.0, MASK_FILL)
-        ones = jnp.ones((HEAD_DIM, PATCH), jnp.bfloat16)
+            spot = (lane >= head * HEAD_DIM) & (lane < (head + 1) * HEAD_DIM) | (lane == 96)
+            keys[side, head * PATCH : (head + 1) * PATCH, :] = keyed * jnp.where(
+                spot, 1.0, 0.0
+            ).astype(jnp.bfloat16)
+        scores[side] = jnp.dot(keys[side], query, preferred_element_type=jnp.float32)
+        alone = 1.0 - jnp.broadcast_to(flags, (PATCH, LANES)).T[0:1, :]
         for head in range(HEADS):
-            here = scores[head * PATCH : (head + 1) * PATCH, :] + bias
-            top = jnp.max(here, axis=0, keepdims=True)
-            exponent = jnp.exp(here - top).astype(jnp.bfloat16)
-            left = jnp.concatenate(
-                [valued[head * HEAD_DIM : (head + 1) * HEAD_DIM, :], ones], axis=0
-            )
-            mixed = jnp.dot(left, exponent, preferred_element_type=jnp.float32)
-            attended[head * HEAD_DIM : (head + 1) * HEAD_DIM, :] = (
-                mixed[:HEAD_DIM] / mixed[HEAD_DIM : HEAD_DIM + 1]
-            )
-        rows[patch * PATCH : (patch + 1) * PATCH, :] = attended[...].T
+            group = slice(head * PATCH, (head + 1) * PATCH)
+            channels = slice(head * HEAD_DIM, (head + 1) * HEAD_DIM)
+            own = jnp.sum(products[channels], axis=0, keepdims=True)
+            for part in range(PATCH // LANES):
+                columns = slice(part * LANES, (part + 1) * LANES)
+                here = scores[side, group, columns]
+                top = jnp.maximum(jnp.max(here, axis=0, keepdims=True), own[:, columns])
+                exponents[side, group, columns] = jnp.exp2(here - top).astype(jnp.bfloat16)
+                extra = jnp.exp2(own[:, columns] - top) * alone[:, columns]
+                diagonal[side, head : head + 1, columns] = extra
+            left = jnp.concatenate([valued[channels], ones], axis=0)
+            mixed = jnp.dot(left, exponents[side, group, :], preferred_element_type=jnp.float32)
+            extra = diagonal[side, head : head + 1, :]
+            upper = mixed[:HEAD_DIM] + extra * valued[channels].astype(jnp.float32)
+            attended[side, channels, :] = upper / (mixed[HEAD_DIM : HEAD_DIM + 1] + extra)
+        rows[patch * PATCH : (patch + 1) * PATCH, :] = attended[side].T
     copy_rows(rows.shape[0], lambda i: i, lambda i: order[i], rows, slots)
     pack_rows(slots, packed, False)
     outbound[...] = packed[...].astype(jnp.bfloat16)
@@ -257,6 +288,18 @@
     )
     value = hidden[...].astype(jnp.float32) + projected
     result[...] = (value * mask[...].astype(jnp.float32)).astype(jnp.bfloat16)
+
+
+def call(body, outputs, in_specs, scratch=(), name=None):
+    return pl.pallas_call(
+        body,
+        out_shape=outputs,
+        in_specs=in_specs,
+        out_specs=tuple(vmem() for _ in outputs),
+        scratch_shapes=list(scratch),
+        compiler_params=pltpu.CompilerParams(vmem_limit_bytes=VMEM_LIMIT),
+        name=name,
+    )
 
 
 def exchange(packed):
@@ -289,32 +332,31 @@
     pair = tokens // spaces
     packed_rows = spaces * ROWS
 
-    def boundary(row_index):
-        start = send_lists[0, 0, row_index, 0] * VOX
-        piece = lax.dynamic_slice(feats[0], (0, start), (96, VOX))
-        flags = lax.dynamic_slice(mask, (0, start), (1, VOX))
-        return piece * flags.astype(bf16)
-
-    low = shifted(boundary(1), "space", 1)
-    high = shifted(boundary(0), "space", -1)
-    table = pl.pallas_call(
+    to_upper, to_lower = call(
+        send_kernel,
+        (jax.ShapeDtypeStruct((96, VOX), bf16),) * 2,
+        [smem()] + [vmem()] * 2,
+        name="send",
+    )(send_lists.reshape(2), feats[0], mask)
+    low = shifted(to_upper, "space", 1)
+    high = shifted(to_lower, "space", -1)
+    table, weights = call(
         layout_kernel,
-        out_shape=jax.ShapeDtypeStruct((tokens, LANES), f32),
-        in_specs=[vmem()] * 2,
-        out_specs=vmem(),
+        (
+            jax.ShapeDtypeStruct((tokens, LANES), f32),
+            jax.ShapeDtypeStruct((3, LANES, 9 * LANES), bf16),
+        ),
+        [smem()] + [vmem()] * 3,
         name="layout",
-    )(feats[0], mask)
-    weights = jnp.pad(conv_w[0].transpose(0, 2, 1), ((0, 0), (0, LANES - 96), (0, LANES - 96)))
-    weights = weights.reshape(3, 9 * LANES, LANES)
-    joined, pooled = pl.pallas_call(
+    )(pool_map.reshape(-1), feats[0], mask, conv_w[0])
+    joined, pooled = call(
         conv_kernel,
-        out_shape=(
+        (
             jax.ShapeDtypeStruct((tokens, LANES), f32),
             jax.ShapeDtypeStruct((blocks * 64, LANES), bf16),
         ),
-        in_specs=[smem()] + [vmem()] * 4,
-        out_specs=(vmem(), vmem()),
-        scratch_shapes=[
+        [smem()] + [vmem()] * 4,
+        [
             pltpu.VMEM((blocks + 3, EDGE, EDGE, EDGE, LANES), f32),
             pltpu.VMEM((3, EDGE + 2, EDGE + 2, EDGE, LANES), f32),
             pltpu.VMEM(((EDGE + 2) * EDGE * EDGE, 9 * LANES), bf16),
@@ -326,40 +368,46 @@
     order_out = send_order[0, 0].reshape(spaces, pair).T.reshape(-1)
     held = patch_order[0, 0]
     order_in = (held % pair) * spaces + held // pair
-    hidden, message = pl.pallas_call(
+    slots, chosen = call(
+        gather_kernel,
+        (
+            jax.ShapeDtypeStruct((tokens, LANES), f32),
+            jax.ShapeDtypeStruct((tokens, 2 * LANES), bf16),
+        ),
+        [smem(), vmem()],
+        name="gather",
+    )(order_out, joined)
+    message = call(
         join_kernel,
-        out_shape=(
-            jax.ShapeDtypeStruct((tokens, LANES), bf16),
-            jax.ShapeDtypeStruct((packed_rows, LANES), bf16),
-        ),
-        in_specs=[smem()] * 2 + [vmem()] * 2,
-        out_specs=(vmem(), vmem()),
-        scratch_shapes=[
-            pltpu.VMEM((blocks * 64, LANES), f32),
-            pltpu.VMEM(((blocks + 1) * 128, LANES), f32),
-            pltpu.VMEM((tokens, LANES), f32),
-            pltpu.VMEM((tokens, LANES), f32),
-            pltpu.VMEM((packed_rows, LANES), f32),
-        ],
+        (jax.ShapeDtypeStruct((packed_rows, LANES), bf16),),
+        [vmem()] * 3,
+        [pltpu.VMEM((tokens, LANES), f32), pltpu.VMEM((packed_rows, LANES), f32)],
         name="join",
-    )(pool_map[0], order_out, joined, coarser)
+    )(slots, chosen, coarser)[0]
+    hidden = call(
+        residual_kernel,
+        (jax.ShapeDtypeStruct((96, tokens), bf16),),
+        [vmem()] * 2,
+        name="residual",
+    )(joined, coarser)[0]
     inbound = exchange(message)
 
     def square(weight):
         return jnp.pad(weight[0], ((0, LANES - 96), (0, LANES - 96)))
 
-    outbound = pl.pallas_call(
+    outbound = call(
         attend_kernel,
-        out_shape=jax.ShapeDtypeStruct((packed_rows, LANES), bf16),
-        in_specs=[smem()] + [vmem()] * 5,
-        out_specs=vmem(),
-        scratch_shapes=[
+        (jax.ShapeDtypeStruct((packed_rows, LANES), bf16),),
+        [smem()] + [vmem()] * 5,
+        [
             pltpu.VMEM((packed_rows, LANES), f32),
             pltpu.VMEM((tokens, LANES), f32),
             pltpu.VMEM((tokens, LANES), f32),
-            pltpu.VMEM((HEADS * PATCH, PATCH), f32),
-            pltpu.VMEM((HEADS * PATCH, LANES), bf16),
-            pltpu.VMEM((LANES, PATCH), f32),
+            pltpu.VMEM((2, HEADS * PATCH, LANES), bf16),
+            pltpu.VMEM((2, HEADS * PATCH, PATCH), f32),
+            pltpu.VMEM((2, HEADS * PATCH, PATCH), bf16),
+            pltpu.VMEM((2, 8, PATCH), f32),
+            pltpu.VMEM((2, LANES, PATCH), f32),
         ],
         name="attend",
     )(
@@ -369,14 +417,13 @@
         square(w_query),
         square(w_key),
         square(w_value),
-    )
+    )[0]
     returned = exchange(outbound)
-    result = pl.pallas_call(
+    result = call(
         finish_kernel,
-        out_shape=jax.ShapeDtypeStruct((96, tokens), bf16),
-        in_specs=[smem()] + [vmem()] * 4,
-        out_specs=vmem(),
-        scratch_shapes=[
+        (jax.ShapeDtypeStruct((96, tokens), bf16),),
+        [smem()] + [vmem()] * 4,
+        [
             pltpu.VMEM((packed_rows, LANES), f32),
             pltpu.VMEM((tokens, LANES), f32),
             pltpu.VMEM((tokens, LANES), f32),
@@ -385,11 +432,11 @@
     )(
         order_out,
         returned,
-        hidden[:, :96].T,
+        hidden,
         mask,
         jnp.pad(w_out[0], ((0, 0), (0, LANES - 96))),
     )
-    return result[None]
+    return result[0][None]
 
 
 def solution(mesh):

time: 130 us -> 117 us (0.900)
  local copies, waits for them, and re-layouts: 12.3 us -> 5.8 us
  Pallas kernels: 27.7 us -> 23.9 us
  other arithmetic: 2.28 us -> 0.15 us
  waiting for transfers between devices: 46 us -> 48 us
    pallas_call x5 -> x8, Pallas kernels: 27.7 us -> 23.9 us  [the longest x1 10.3 us: shards(): call(attend_kernel, (jax.ShapeDtypeStruct((packed_rows, LANES), bf16),),...]
    all_to_all x2, waiting for transfers between devices: 45.9 us -> 48 us  [exchange(): lax.all_to_all(tiles, 'space', split_axis=0, concat_axis=0, tiled=True)]
    pad x3, local copies, waits for them, and re-layouts: 1.85 us -> 0.03 us  [square(): return jnp.pad(weight[0], ((0, LANES - 96), (0, LANES - 96)))]
    slice x1 -> x0, local copies, waits for them, and re-layouts: 1.38 us -> none  [boundary(): start = send_lists[0, 0, row_index, 0] * VOX]
    unnamed x35 -> x31, local copies, waits for them, and re-layouts: 5.62 us -> 5.51 us
  transfers between devices with their start and end apart: 5 -> 5, of which waited for: 3 -> 2; matrix products, arithmetic and copies ran while one was open for 7% -> 0% of each run, Pallas kernels for 2% -> 3%
where the time goes in v2:
time: 117 us; the launch traced here: 116 us
  waiting for transfers between devices  48 us (41%)
  starting transfers between devices  38 us (32%)
  Pallas kernels  23.9 us (20%)
  local copies, waits for them, and re-layouts  5.8 us (5%)
    all_to_all x2, waiting for transfers between devices, exchange(): lax.all_to_all(tiles, 'space', split_axis=0, concat_axis=0, tiled=True)  48 us
    all_to_all x2, starting transfers between devices, exchange(): lax.all_to_all(tiles, 'space', split_axis=0, concat_axis=0, tiled=True)  26.3 us
    ppermute x3, starting transfers between devices, shifted(): return lax.ppermute(block, axis, route)  11.7 us
    pallas_call x1, Pallas kernels, shards(): call(attend_kernel, (jax.ShapeDtypeStruct((packed_rows, LANES), bf16),),...  10.3 us
    unnamed x31, local copies, waits for them, and re-layouts  5.51 us
    pallas_call x1, Pallas kernels, shards(): call(conv_kernel, (jax.ShapeDtypeStruct((tokens, LANES), f32), jax.ShapeD...  4.14 us
    pallas_call x1, Pallas kernels, shards(): call(finish_kernel, (jax.ShapeDtypeStruct((96, tokens), bf16),), [smem()]...  3.49 us
    pallas_call x1, Pallas kernels, shards(): call(gather_kernel, (jax.ShapeDtypeStruct((tokens, LANES), f32), jax.Shap...  2.54 us
  transfers between devices with their start and end apart: 5, of which 2 were waited for; matrix products, arithmetic and copies ran while one was open for 0% of the time, Pallas kernels for 3%

profile of v2, /device:TPU:1, one launch (start us, length us, event | category | flops | bytes accessed | tf_op | source)
XLA Modules:
  0.0 116.1 jit_solution(16559043703613922840)
XLA Ops:
  0.0 0.7 copy-done.5
  0.7 1.0 copy-done
  1.6 0.7 copy-done.3
  2.3 0.6 send.1
  2.9 4.9 %collective-permute-start = (bf16[96,512]{1,0:T(8,128)(2,1)S(1)}, bf16[96,512]{1,0:T(8,128)(2,1)S(1)}, u32[]{:S(2)}, u32[]{:S(2)}) collective-permute-start(bf16[96,512]{1,0:T(8,128)(2,1)S(1)} %get-tuple-element.14), channel_id=1, source_target_pairs={{0,1},{1,2},{2,3},{3,4},{4,5},{5,6},{6,7},{7,8},{8,9},{9,10},{10,1... | collective-permute-start | bytes 294920 | tf_op jit(solution)/shard_map/ppermute | solution.py:26
  7.9 5.1 %collective-permute-start.1 = (bf16[96,512]{1,0:T(8,128)(2,1)S(1)}, bf16[96,512]{1,0:T(8,128)(2,1)S(1)}, u32[]{:S(2)}, u32[]{:S(2)}) collective-permute-start(bf16[96,512]{1,0:T(8,128)(2,1)S(1)} %get-tuple-element.15), channel_id=1, source_target_pairs={{1,0},{2,1},{3,2},{4,3},{5,4},{6,5},{7,6},{8,7},{9,8},{10,9},{11,1... | collective-permute-start | bytes 294920 | tf_op jit(solution)/shard_map/ppermute | solution.py:26
  13.0 0.1 reshape.29.octants
  13.1 1.1 copy-done.2
  14.2 1.0 layout.1
  15.2 4.1 %conv.1 = (f32[1536,128]{1,0:T(8,128)S(1)}, bf16[192,128]{1,0:T(8,128)(2,1)S(1)}) custom-call(s32[3,26]{1,0:T(4,128)S(1)} %bitcast.24, f32[1536,128]{1,0:T(8,128)S(1)} %get-tuple-element.13.own, bf16[96,512]{1,0:T(8,128)(2,1)S(1)} %collective-permute-done.low, bf16[96,512]{1,0:T(8,128)(2,1)S(1)} %collective-permute-done.1.high, ...), custom_call_target="tpu_custom_call" | custom-call | tf_op jit(solution)/shard_map/conv/pallas_call | solution.py:352
  19.4 1.7 %collective-permute-start.2 = (bf16[192,128]{1,0:T(8,128)(2,1)S(1)}, bf16[192,128]{1,0:T(8,128)(2,1)S(1)}, u32[]{:S(2)}, u32[]{:S(2)}) collective-permute-start(bf16[192,128]{1,0:T(8,128)(2,1)S(1)} %get-tuple-element.20), channel_id=1, source_target_pairs={{0,128},{128,256},{256,384},{1,129},{129,257},{257,385},{2,130},{1... | collective-permute-start | bytes 147464 | tf_op jit(solution)/shard_map/ppermute | solution.py:26
  21.1 0.1 reshape_squeeze.3
  21.3 2.5 %gather.1 = (f32[1536,128]{1,0:T(8,128)S(1)}, bf16[1536,256]{1,0:T(8,128)(2,1)S(1)}) custom-call(s32[1536]{0:T(1024)S(1)} %bitcast.22, f32[1536,128]{1,0:T(8,128)S(1)} %get-tuple-element.17.joined), custom_call_target="tpu_custom_call" | custom-call | tf_op jit(solution)/shard_map/gather/pallas_call | solution.py:371
  23.8 1.3 %join.1 = bf16[1280,128]{1,0:T(8,128)(2,1)} custom-call(f32[1536,128]{1,0:T(8,128)S(1)} %get-tuple-element.18.slots, bf16[1536,256]{1,0:T(8,128)(2,1)S(1)} %get-tuple-element.19.chosen, bf16[192,128]{1,0:T(8,128)(2,1)S(1)} %collective-permute-done.2.coarser), custom_call_target="tpu_custom_call" | custom-call | tf_op jit(solution)/shard_map/join/pallas_call | solution.py:380
  25.2 19.2 %all-to-all-start = ((bf16[640,2,128]{2,1,0:T(2,128)(2,1)}), bf16[640,2,128]{2,1,0:T(2,128)(2,1)S(1)}, u32[]{:S(2)}, u32[]{:S(2)}) async-start(bf16[640,2,128]{2,1,0:T(2,128)(2,1)} %bitcast.5), calls=%async_computation | async-start | bytes 655360 | tf_op jit(solution)/shard_map/all_to_all | solution.py:308
  44.4 0.7 copy-done.7
  45.1 0.7 copy-done.8
  45.8 0.6 copy-done.14
  46.6 23.1 %all-to-all-done = bf16[640,2,128]{2,1,0:T(2,128)(2,1)S(1)} async-done(((bf16[640,2,128]{2,1,0:T(2,128)(2,1)}), bf16[640,2,128]{2,1,0:T(2,128)(2,1)S(1)}, u32[]{:S(2)}, u32[]{:S(2)}) %all-to-all-start) | async-done | bytes 327712 | tf_op jit(solution)/shard_map/all_to_all | solution.py:308
  69.7 10.3 %attend.1 = bf16[1280,128]{1,0:T(8,128)(2,1)} custom-call(s32[1536]{0:T(1024)S(1)} %fusion.1.order, bf16[1280,128]{1,0:T(8,128)(2,1)S(1)} %bitcast.17, f32[1,128]{1,0:T(1,128)S(1)} %pad_convert_fusion.gain, bf16[128,128]{1,0:T(8,128)(2,1)S(1)} %pad.22.w_query, bf16[128,128]{1,0:T(8,128)(2,1)S(1)} %pad.23.w_key, bf16[128,128]{1,0:T(8,128)(2,1)S(1)} %pad.24.w_value), custom_call_target="tpu_custom_call" | custom-call | tf_op jit(solution)/shard_map/attend/pallas_call | solution.py:398
  80.0 7.1 %all-to-all-start.1 = ((bf16[640,2,128]{2,1,0:T(2,128)(2,1)}), bf16[640,2,128]{2,1,0:T(2,128)(2,1)S(1)}, u32[]{:S(2)}, u32[]{:S(2)}) async-start(bf16[640,2,128]{2,1,0:T(2,128)(2,1)} %bitcast.10), calls=%async_computation.1 | async-start | bytes 655360 | tf_op jit(solution)/shard_map/all_to_all | solution.py:308
  87.1 0.5 residual.1.hidden
  87.7 24.9 %all-to-all-done.1 = bf16[640,2,128]{2,1,0:T(2,128)(2,1)S(1)} async-done(((bf16[640,2,128]{2,1,0:T(2,128)(2,1)}), bf16[640,2,128]{2,1,0:T(2,128)(2,1)S(1)}, u32[]{:S(2)}, u32[]{:S(2)}) %all-to-all-start.1) | async-done | bytes 327712 | tf_op jit(solution)/shard_map/all_to_all | solution.py:308
  112.6 3.5 %finish.1 = bf16[96,1536]{1,0:T(8,128)(2,1)} custom-call(s32[1536]{0:T(1024)S(1)} %bitcast.23, bf16[1280,128]{1,0:T(8,128)(2,1)S(1)} %bitcast.18, bf16[96,1536]{1,0:T(8,128)(2,1)S(1)} %residual.1.hidden, s32[1,1536]{1,0:T(1,128)S(1)} %copy-done.4, bf16[96,128]{1,0:T(8,128)(2,1)S(1)} %pad.25.w_out), custom_call_target="tpu_custom_call" | custom-call | tf_op jit(solution)/shard_map/finish/pallas_call | solution.py:422
  (38 shorter events, 0.3 us)
Async XLA Ops:
  0.0 0.7 copy-start.5
  0.7 1.0 copy-start
  1.6 0.7 copy-start.3
  2.3 10.8 %copy-start.1 = (bf16[1,96,1536]{2,1,0:T(8,128)(2,1)S(1)}, bf16[1,96,1536]{2,1,0:T(8,128)(2,1)}, u32[]{:S(2)}) copy-start(bf16[1,96,1536]{2,1,0:T(8,128)(2,1)} %param.13) | copy-start | bytes 884740
  2.9 10.1 %copy-start.13 = (s32[1,3,8]{2,0,1:T(1,128)S(1)}, s32[1,3,8]{2,0,1:T(1,128)}, u32[]{:S(2)}) copy-start(s32[1,3,8]{2,0,1:T(1,128)} %param.18) | copy-start | bytes 292
  2.9 10.2 %copy-start.12 = (s32[1,3,26]{2,0,1:T(1,128)S(1)}, s32[1,3,26]{2,0,1:T(1,128)}, u32[]{:S(2)}) copy-start(s32[1,3,26]{2,0,1:T(1,128)} %param.16) | copy-start | bytes 940
  2.9 12.3 %collective-permute-start = (bf16[96,512]{1,0:T(8,128)(2,1)S(1)}, bf16[96,512]{1,0:T(8,128)(2,1)S(1)}, u32[]{:S(2)}, u32[]{:S(2)}) collective-permute-start(bf16[96,512]{1,0:T(8,128)(2,1)S(1)} %get-tuple-element.14), channel_id=1, source_target_pairs={{0,1},{1,2},{2,3},{3,4},{4,5},{5,6},{6,7},{7,8},{8,9},{9,10},{10,1... | collective-permute-start | bytes 294920 | tf_op jit(solution)/shard_map/ppermute | solution.py:26
  7.9 5.3 %copy-start.4 = (s32[1,1536]{1,0:T(1,128)S(1)}, s32[1,1536]{1,0:T(1,128)}, u32[]{:S(2)}) copy-start(s32[1,1536]{1,0:T(1,128)} %mask.5) | copy-start | bytes 18436
  7.9 7.4 %collective-permute-start.1 = (bf16[96,512]{1,0:T(8,128)(2,1)S(1)}, bf16[96,512]{1,0:T(8,128)(2,1)S(1)}, u32[]{:S(2)}, u32[]{:S(2)}) collective-permute-start(bf16[96,512]{1,0:T(8,128)(2,1)S(1)} %get-tuple-element.15), channel_id=1, source_target_pairs={{1,0},{2,1},{3,2},{4,3},{5,4},{6,5},{7,6},{8,7},{9,8},{10,9},{11,1... | collective-permute-start | bytes 294920 | tf_op jit(solution)/shard_map/ppermute | solution.py:26
  13.1 1.1 copy-start.2
  15.2 5.8 %copy-start.11 = (s32[1,1,1536]{2,1,0:T(1,128)S(1)}, s32[1,1,1536]{2,1,0:T(1,128)}, u32[]{:S(2)}) copy-start(s32[1,1,1536]{2,1,0:T(1,128)} %param.19) | copy-start | bytes 18436
  19.4 4.4 %collective-permute-start.2 = (bf16[192,128]{1,0:T(8,128)(2,1)S(1)}, bf16[192,128]{1,0:T(8,128)(2,1)S(1)}, u32[]{:S(2)}, u32[]{:S(2)}) collective-permute-start(bf16[192,128]{1,0:T(8,128)(2,1)S(1)} %get-tuple-element.20), channel_id=1, source_target_pairs={{0,128},{128,256},{256,384},{1,129},{129,257},{257,385},{2,130},{1... | collective-permute-start | bytes 147464 | tf_op jit(solution)/shard_map/ppermute | solution.py:26
  25.2 19.2 %copy-start.6 = (bf16[1,96,96]{2,1,0:T(8,128)(2,1)S(1)}, bf16[1,96,96]{2,1,0:T(8,128)(2,1)}, u32[]{:S(2)}) copy-start(bf16[1,96,96]{2,1,0:T(8,128)(2,1)} %param.22) | copy-start | bytes 55300
  25.2 44.5 %all-to-all-start = ((bf16[640,2,128]{2,1,0:T(2,128)(2,1)}), bf16[640,2,128]{2,1,0:T(2,128)(2,1)S(1)}, u32[]{:S(2)}, u32[]{:S(2)}) async-start(bf16[640,2,128]{2,1,0:T(2,128)(2,1)} %bitcast.5), calls=%async_computation | async-start | bytes 655360 | tf_op jit(solution)/shard_map/all_to_all | solution.py:308
  44.4 0.7 copy-start.7
  45.1 0.7 copy-start.8
  45.1 1.4 %copy-start.10 = (s32[1,1,1536]{2,1,0:T(1,128)S(1)}, s32[1,1,1536]{2,1,0:T(1,128)}, u32[]{:S(2)}) copy-start(s32[1,1,1536]{2,1,0:T(1,128)} %param.20) | copy-start | bytes 18436
  45.8 0.7 copy-start.14
  80.0 7.1 %copy-start.9 = (bf16[1,96,96]{2,1,0:T(8,128)(2,1)S(1)}, bf16[1,96,96]{2,1,0:T(8,128)(2,1)}, u32[]{:S(2)}) copy-start(bf16[1,96,96]{2,1,0:T(8,128)(2,1)} %param.25) | copy-start | bytes 55300
  80.0 32.6 %all-to-all-start.1 = ((bf16[640,2,128]{2,1,0:T(2,128)(2,1)}), bf16[640,2,128]{2,1,0:T(2,128)(2,1)S(1)}, u32[]{:S(2)}, u32[]{:S(2)}) async-start(bf16[640,2,128]{2,1,0:T(2,128)(2,1)} %bitcast.10), calls=%async_computation.1 | async-start | bytes 655360 | tf_op jit(solution)/shard_map/all_to_all | solution.py:308

commit v3 on v2

--- a/solution.py
+++ b/solution.py
@@ -1,3 +1,4 @@
+import functools
 import math
 
 import jax
@@ -18,6 +19,7 @@
 ROWS = 10
 CONTRACT_LAST = (((1,), (1,)), ((), ()))
 VMEM_LIMIT = 24 << 20
+FIRST_PEER = 80
 
 
 def shifted(block, axis, distance):
@@ -26,6 +28,14 @@
     return lax.ppermute(block, axis, route)
 
 
+def swapped(block, axis, parity):
+    count = lax.axis_size(axis)
+    route = []
+    for i in range(parity, count - 1, 2):
+        route += [(i, i + 1), (i + 1, i)]
+    return lax.ppermute(block, axis, route)
+
+
 def vmem():
     return pl.BlockSpec(memory_space=pltpu.VMEM)
 
@@ -38,17 +48,19 @@
     return lax.broadcasted_iota(jnp.int32, shape, len(shape) - 1)
 
 
-def copy_rows(count, read_index, write_index, src, dst):
-    step = 16
-
-    def body(outer, carry):
-        base = outer * step
-        for inner in range(step):
-            i = base + inner
-            dst[pl.ds(write_index(i), 1), :] = src[pl.ds(read_index(i), 1), :]
-        return carry
-
-    lax.fori_loop(0, count // step, body, 0)
+def gather_rows(read_index, src, dst):
+    for i in range(dst.shape[0]):
+        dst[i : i + 1, :] = src[pl.ds(read_index(i), 1), :]
+
+
+def scatter_rows(write_index, src, dst):
+    for i in range(src.shape[0]):
+        dst[pl.ds(write_index(i), 1), :] = src[i : i + 1, :]
+
+
+def sent_token(order, first, peers):
+    pair = order.shape[1] // peers
+    return lambda i: order[0, (i % peers + first) % peers * pair + i // peers]
 
 
 def pack_rows(slots, packed, with_mask):
@@ -89,11 +101,20 @@
             slots[t * peers : (t + 1) * peers, :] = value
 
 
-def send_kernel(lists, feats, mask, to_upper, to_lower):
-    for out, row_index in ((to_upper, 1), (to_lower, 0)):
-        here = pl.ds(pl.multiple_of(lists[row_index] * VOX, VOX), VOX)
-        flags = mask[:, here].astype(jnp.float32)
-        out[...] = (feats[:, here].astype(jnp.float32) * flags).astype(jnp.bfloat16)
+def send_kernel(lists, feats, mask, across, inside, slots, block, flags, ready):
+    copies = [
+        pltpu.make_async_copy(source, target, ready.at[i])
+        for i, (source, target) in enumerate(((lists, slots), (feats, block), (mask, flags)))
+    ]
+    for copy in copies:
+        copy.start()
+    for copy in copies:
+        copy.wait()
+    odd = lax.rem(lax.axis_index("space"), 2)
+    for out, row_index in ((across, odd), (inside, 1 - odd)):
+        here = pl.ds(pl.multiple_of(slots[0, row_index] * VOX, VOX), VOX)
+        shown = flags[:, here].astype(jnp.float32)
+        out[...] = (block[:, here].astype(jnp.float32) * shown).astype(jnp.bfloat16)
 
 
 def layout_kernel(octants, feats, mask, taps, table, weights):
@@ -104,8 +125,8 @@
     x, y, z = (token >> 6) & 7, (token >> 3) & 7, token & 7
     octant = ((token >> 9) << 3) + ((x >> 2) << 2) + ((y >> 2) << 1) + (z >> 2)
     slot = jnp.full((1, tokens), 3, jnp.int32)
-    for k in range(octants.shape[0]):
-        slot = jnp.where(octant == k, octants[k], slot)
+    for k in range(octants.shape[0] * 8):
+        slot = jnp.where(octant == k, octants[k // 8, 0, k % 8], slot)
     within = ((x & 3) << 4) + ((y & 3) << 2) + (z & 3)
     child = jnp.where((slot < 3) & (mask[...] > 0), slot * 64 + within, 255).astype(jnp.float32)
     row = lax.broadcasted_iota(jnp.int32, (LANES - 96, tokens), 0)
@@ -117,12 +138,13 @@
         weights[k // 9, 0:96, at : at + 96] = taps[k]
 
 
-def conv_kernel(rules, own, low, high, weights, joined, pooled, table, padded, views, halves):
+def conv_kernel(rules, own, across, inside, weights, joined, pooled, table, padded, views, halves):
     blocks = own.shape[0] // VOX
     pad_lanes = jnp.zeros((LANES - 96, VOX), jnp.float32)
     for b in range(blocks):
         table[b] = own[b * VOX : (b + 1) * VOX, :].reshape(EDGE, EDGE, EDGE, LANES)
-    for spot, ref in ((blocks, low), (blocks + 1, high)):
+    odd = lax.rem(lax.axis_index("space"), 2)
+    for spot, ref in ((blocks + odd, across), (blocks + 1 - odd, inside)):
         values = jnp.concatenate([ref[...].astype(jnp.float32), pad_lanes], axis=0).T
         table[spot] = values.reshape(EDGE, EDGE, EDGE, LANES)
     table[blocks + 2] = jnp.zeros((EDGE, EDGE, EDGE, LANES), jnp.float32)
@@ -140,7 +162,7 @@
             k = 9 * (dx + 1) + 3 * (dy + 1) + dz + 1
             if k == 13:
                 return b
-            return rules[b, k if k < 13 else k - 1]
+            return rules[b, 0, k if k < 13 else k - 1]
 
         for dx in (-1, 0, 1):
             sx, tx = span(dx)
@@ -195,8 +217,8 @@
     return rows + jnp.dot(chosen, below, preferred_element_type=jnp.float32)
 
 
-def gather_kernel(order, joined, slots, chosen):
-    copy_rows(slots.shape[0], lambda i: order[i], lambda i: i, joined, slots)
+def gather_kernel(first, peers, order, joined, slots, chosen):
+    gather_rows(sent_token(order, first, peers), joined, slots)
     chosen[...] = child_matrix(slots[...])
 
 
@@ -220,7 +242,7 @@
 ):
     packed[...] = inbound[...].astype(jnp.float32)
     unpack_rows(packed, slots, True)
-    copy_rows(rows.shape[0], lambda i: order[i], lambda i: i, slots, rows)
+    gather_rows(lambda i: order[0, i], slots, rows)
     lane = lane_of((1, LANES))
     inside = lane < 96
     channel = lax.broadcasted_iota(jnp.int32, (LANES, PATCH), 0)
@@ -271,15 +293,15 @@
             upper = mixed[:HEAD_DIM] + extra * valued[channels].astype(jnp.float32)
             attended[side, channels, :] = upper / (mixed[HEAD_DIM : HEAD_DIM + 1] + extra)
         rows[patch * PATCH : (patch + 1) * PATCH, :] = attended[side].T
-    copy_rows(rows.shape[0], lambda i: i, lambda i: order[i], rows, slots)
+    scatter_rows(lambda i: order[0, i], rows, slots)
     pack_rows(slots, packed, False)
     outbound[...] = packed[...].astype(jnp.bfloat16)
 
 
-def finish_kernel(order, returned, hidden, mask, w_out, result, packed, slots, rows):
+def finish_kernel(first, peers, order, returned, hidden, mask, w_out, result, packed, slots, rows):
     packed[...] = returned[...].astype(jnp.float32)
     unpack_rows(packed, slots, False)
-    copy_rows(rows.shape[0], lambda i: i, lambda i: order[i], slots, rows)
+    scatter_rows(sent_token(order, first, peers), slots, rows)
     projected = lax.dot_general(
         w_out[...],
         rows[...].astype(jnp.bfloat16),
@@ -302,12 +324,13 @@
     )
 
 
-def exchange(packed):
+def exchange(packed, first):
     spaces = lax.axis_size("space")
     tiles = packed.reshape(packed.shape[0] // 2, 2, LANES)
-    return lax.all_to_all(tiles, "space", split_axis=0, concat_axis=0, tiled=True).reshape(
-        packed.shape
-    )
+    peers = [[(first + i) % spaces for i in range(spaces)]]
+    return lax.all_to_all(
+        tiles, "space", split_axis=0, concat_axis=0, axis_index_groups=peers, tiled=True
+    ).reshape(packed.shape)
 
 
 def shards(
@@ -332,14 +355,23 @@
     pair = tokens // spaces
     packed_rows = spaces * ROWS
 
-    to_upper, to_lower = call(
+    def in_hbm(array):
+        return pltpu.with_memory_space_constraint(array, pltpu.HBM)
+
+    across, inside = call(
         send_kernel,
         (jax.ShapeDtypeStruct((96, VOX), bf16),) * 2,
-        [smem()] + [vmem()] * 2,
+        [pl.BlockSpec(memory_space=pltpu.HBM)] * 3,
+        [
+            pltpu.SMEM((1, 2), jnp.int32),
+            pltpu.VMEM((96, tokens), bf16),
+            pltpu.VMEM((1, tokens), jnp.int32),
+            pltpu.SemaphoreType.DMA((3,)),
+        ],
         name="send",
-    )(send_lists.reshape(2), feats[0], mask)
-    low = shifted(to_upper, "space", 1)
-    high = shifted(to_lower, "space", -1)
+    )(in_hbm(send_lists.reshape(1, 2)), in_hbm(feats[0]), in_hbm(mask))
+    across = swapped(across, "space", 1)
+    inside = swapped(inside, "space", 0)
     table, weights = call(
         layout_kernel,
         (
@@ -348,7 +380,7 @@
         ),
         [smem()] + [vmem()] * 3,
         name="layout",
-    )(pool_map.reshape(-1), feats[0], mask, conv_w[0])
+    )(pool_map.reshape(blocks, 1, 8), feats[0], mask, conv_w[0])
     joined, pooled = call(
         conv_kernel,
         (
@@ -363,13 +395,14 @@
             pltpu.VMEM((16 * EDGE, LANES), f32),
         ],
         name="conv",
-    )(rules[0], table, low, high, weights)
+    )(rules.reshape(blocks, 1, 26), table, across, inside, weights)
     coarser = shifted(pooled, "section", 1)
-    order_out = send_order[0, 0].reshape(spaces, pair).T.reshape(-1)
-    held = patch_order[0, 0]
-    order_in = (held % pair) * spaces + held // pair
+    first = FIRST_PEER % spaces
+    order_out = send_order.reshape(1, tokens)
+    held = patch_order.reshape(1, tokens)
+    order_in = (held % pair) * spaces + (held // pair + (spaces - first)) % spaces
     slots, chosen = call(
-        gather_kernel,
+        functools.partial(gather_kernel, first, spaces),
         (
             jax.ShapeDtypeStruct((tokens, LANES), f32),
             jax.ShapeDtypeStruct((tokens, 2 * LANES), bf16),
@@ -390,7 +423,7 @@
         [vmem()] * 2,
         name="residual",
     )(joined, coarser)[0]
-    inbound = exchange(message)
+    inbound = exchange(message, first)
 
     def square(weight):
         return jnp.pad(weight[0], ((0, LANES - 96), (0, LANES - 96)))
@@ -418,9 +451,9 @@
         square(w_key),
         square(w_value),
     )[0]
-    returned = exchange(outbound)
+    returned = exchange(outbound, first)
     result = call(
-        finish_kernel,
+        functools.partial(finish_kernel, first, spaces),
         (jax.ShapeDtypeStruct((96, tokens), bf16),),
         [smem()] + [vmem()] * 4,
         [

time: 117 us -> 104 us (0.89)
  waiting for transfers between devices: 48 us -> 26.7 us
  starting transfers between devices: 38 us -> 52.1 us
  Pallas kernels: 23.9 us -> 20.2 us
  local copies, waits for them, and re-layouts: 5.8 us -> 3.91 us
    all_to_all x2, waiting for transfers between devices: 48 us -> 26.7 us  [exchange(): lax.all_to_all(tiles, 'space', split_axis=0, concat_axis=0, axis_index_gr...]
    all_to_all x2, starting transfers between devices: 26.3 us -> 41.4 us  [exchange(): lax.all_to_all(tiles, 'space', split_axis=0, concat_axis=0, axis_index_gr...]
    ppermute x3 -> x1, starting transfers between devices: 11.7 us -> 1.29 us  [shifted(): return lax.ppermute(block, axis, route)]
    ppermute x0 -> x2, starting transfers between devices: none -> 9.41 us  [swapped(): return lax.ppermute(block, axis, route)]
    pallas_call x1, Pallas kernels: 10.3 us -> 7.75 us  [shards(): call(attend_kernel, (jax.ShapeDtypeStruct((packed_rows, LANES), bf16),),...]
    unnamed x31 -> x24, local copies, waits for them, and re-layouts: 5.51 us -> 3.87 us
where the time goes in v3:
time: 104 us; the launch traced here: 103 us
  starting transfers between devices  52.1 us (50%)
  waiting for transfers between devices  26.7 us (26%)
  Pallas kernels  20.2 us (19%)
  local copies, waits for them, and re-layouts  3.91 us (4%)
    all_to_all x2, starting transfers between devices, exchange(): lax.all_to_all(tiles, 'space', split_axis=0, concat_axis=0, axis_index_gr...  41.4 us
    all_to_all x2, waiting for transfers between devices, exchange(): lax.all_to_all(tiles, 'space', split_axis=0, concat_axis=0, axis_index_gr...  26.7 us
    ppermute x2, starting transfers between devices, swapped(): return lax.ppermute(block, axis, route)  9.41 us
    pallas_call x1, Pallas kernels, shards(): call(attend_kernel, (jax.ShapeDtypeStruct((packed_rows, LANES), bf16),),...  7.75 us
    pallas_call x1, Pallas kernels, shards(): call(conv_kernel, (jax.ShapeDtypeStruct((tokens, LANES), f32), jax.ShapeD...  4.18 us
    unnamed x24, local copies, waits for them, and re-layouts  3.87 us
    pallas_call x1, Pallas kernels, shards(): call(functools.partial(finish_kernel, first, spaces), (jax.ShapeDtypeStru...  2.51 us
  transfers between devices with their start and end apart: 5, of which 2 were waited for; matrix products, arithmetic and copies ran while one was open for 0% of the time, Pallas kernels for 3%

profile of v3, /device:TPU:1, one launch (start us, length us, event | category | flops | bytes accessed | tf_op | source)
XLA Modules:
  0.0 103.2 jit_solution(6481679823075667301)
XLA Ops:
  0.0 1.1 %send.1 = (bf16[96,512]{1,0:T(8,128)(2,1)S(1)}, bf16[96,512]{1,0:T(8,128)(2,1)S(1)}) custom-call(s32[1,2]{1,0:T(1,128)} %bitcast.43, bf16[96,1536]{1,0:T(8,128)(2,1)} %bitcast.32, s32[1,1536]{1,0:T(1,128)} %mask.5), custom_call_target="tpu_custom_call" | custom-call | tf_op jit(solution)/shard_map/send/pallas_call | solution.py:361
  1.1 0.0 copy-start.2
  1.1 4.9 %collective-permute-start = (bf16[96,512]{1,0:T(8,128)(2,1)S(1)}, bf16[96,512]{1,0:T(8,128)(2,1)S(1)}, u32[]{:S(2)}, u32[]{:S(2)}) collective-permute-start(bf16[96,512]{1,0:T(8,128)(2,1)S(1)} %get-tuple-element.14), channel_id=1, source_target_pairs={{1,2},{2,1},{3,4},{4,3},{5,6},{6,5},{7,8},{8,7},{9,10},{10,9},{11,... | collective-permute-start | bytes 294920 | tf_op jit(solution)/shard_map/ppermute | solution.py:36
  6.1 0.0 copy-start.4
  6.1 4.5 %collective-permute-start.1 = (bf16[96,512]{1,0:T(8,128)(2,1)S(1)}, bf16[96,512]{1,0:T(8,128)(2,1)S(1)}, u32[]{:S(2)}, u32[]{:S(2)}) collective-permute-start(bf16[96,512]{1,0:T(8,128)(2,1)S(1)} %get-tuple-element.15), channel_id=1, source_target_pairs={{0,1},{1,0},{2,3},{3,2},{4,5},{5,4},{6,7},{7,6},{8,9},{9,8},{10,11... | collective-permute-start | bytes 294920 | tf_op jit(solution)/shard_map/ppermute | solution.py:36
  10.6 1.1 %copy-done.1 = bf16[1,27,96,96]{3,2,1,0:T(8,128)(2,1)S(1)} copy-done((bf16[1,27,96,96]{3,2,1,0:T(8,128)(2,1)S(1)}, bf16[1,27,96,96]{3,2,1,0:T(8,128)(2,1)}, u32[]{:S(2)}) %copy-start.1) | copy-done | bytes 497688
  11.7 1.0 layout.1
  12.7 0.7 copy-done.5
  13.4 4.2 %conv.1 = (f32[1536,128]{1,0:T(8,128)S(1)}, bf16[192,128]{1,0:T(8,128)(2,1)S(1)}) custom-call(s32[3,1,26]{2,1,0:T(1,128)S(1)} %bitcast.38, f32[1536,128]{1,0:T(8,128)S(1)} %get-tuple-element.13.own, bf16[96,512]{1,0:T(8,128)(2,1)S(1)} %collective-permute-done.across, bf16[96,512]{1,0:T(8,128)(2,1)S(1)} %collective-permute-done.1.inside, ...), custom_call_target="tpu_custom_call" | custom-call | tf_op jit(solution)/shard_map/conv/pallas_call | solution.py:384
  17.6 1.3 %collective-permute-start.2 = (bf16[192,128]{1,0:T(8,128)(2,1)S(1)}, bf16[192,128]{1,0:T(8,128)(2,1)S(1)}, u32[]{:S(2)}, u32[]{:S(2)}) collective-permute-start(bf16[192,128]{1,0:T(8,128)(2,1)S(1)} %get-tuple-element.20), channel_id=1, source_target_pairs={{0,128},{128,256},{256,384},{1,129},{129,257},{257,385},{2,130},{1... | collective-permute-start | bytes 147464 | tf_op jit(solution)/shard_map/ppermute | solution.py:28
  18.9 1.9 %gather.1 = (f32[1536,128]{1,0:T(8,128)S(1)}, bf16[1536,256]{1,0:T(8,128)(2,1)S(1)}) custom-call(s32[1,1536]{1,0:T(1,128)S(1)} %bitcast.35, f32[1536,128]{1,0:T(8,128)S(1)} %get-tuple-element.17.joined), custom_call_target="tpu_custom_call" | custom-call | tf_op jit(solution)/shard_map/gather/pallas_call | solution.py:404
  20.8 1.3 %join.1 = bf16[1280,128]{1,0:T(8,128)(2,1)} custom-call(f32[1536,128]{1,0:T(8,128)S(1)} %get-tuple-element.18.slots, bf16[1536,256]{1,0:T(8,128)(2,1)S(1)} %get-tuple-element.19.chosen, bf16[192,128]{1,0:T(8,128)(2,1)S(1)} %collective-permute-done.2.coarser), custom_call_target="tpu_custom_call" | custom-call | tf_op jit(solution)/shard_map/join/pallas_call | solution.py:413
  22.1 23.8 %all-to-all-start = ((bf16[640,2,128]{2,1,0:T(2,128)(2,1)}), bf16[640,2,128]{2,1,0:T(2,128)(2,1)S(1)}, u32[]{:S(2)}, u32[]{:S(2)}) async-start(bf16[640,2,128]{2,1,0:T(2,128)(2,1)} %bitcast.9), calls=%async_computation | async-start | bytes 655360 | tf_op jit(solution)/shard_map/all_to_all | solution.py:331
  45.9 0.0 copy-start.7
  45.9 0.7 copy-done.7
  46.6 0.7 copy-done.8
  47.4 0.6 copy-done.11
  48.0 0.1 fusion.1.order
  48.1 12.5 %all-to-all-done = bf16[640,2,128]{2,1,0:T(2,128)(2,1)S(1)} async-done(((bf16[640,2,128]{2,1,0:T(2,128)(2,1)}), bf16[640,2,128]{2,1,0:T(2,128)(2,1)S(1)}, u32[]{:S(2)}, u32[]{:S(2)}) %all-to-all-start) | async-done | bytes 327712 | tf_op jit(solution)/shard_map/all_to_all | solution.py:331
  60.7 7.7 %attend.1 = bf16[1280,128]{1,0:T(8,128)(2,1)} custom-call(s32[1,1536]{1,0:T(1,128)S(1)} %fusion.1.order, bf16[1280,128]{1,0:T(8,128)(2,1)S(1)} %bitcast.30, f32[1,128]{1,0:T(1,128)S(1)} %pad_convert_fusion.gain, bf16[128,128]{1,0:T(8,128)(2,1)S(1)} %pad.22.w_query, bf16[128,128]{1,0:T(8,128)(2,1)S(1)} %pad.23.w_key, bf16[128,128]{1,0:T(8,128)(2,1)S(1)} %pad.24.w_value), custom_call_target="tpu_custom_call" | custom-call | tf_op jit(solution)/shard_map/attend/pallas_call | solution.py:431
  68.4 17.6 %all-to-all-start.1 = ((bf16[640,2,128]{2,1,0:T(2,128)(2,1)}), bf16[640,2,128]{2,1,0:T(2,128)(2,1)S(1)}, u32[]{:S(2)}, u32[]{:S(2)}) async-start(bf16[640,2,128]{2,1,0:T(2,128)(2,1)} %bitcast.14), calls=%async_computation.1 | async-start | bytes 655360 | tf_op jit(solution)/shard_map/all_to_all | solution.py:331
  86.0 0.5 residual.1.hidden
  86.5 14.2 %all-to-all-done.1 = bf16[640,2,128]{2,1,0:T(2,128)(2,1)S(1)} async-done(((bf16[640,2,128]{2,1,0:T(2,128)(2,1)}), bf16[640,2,128]{2,1,0:T(2,128)(2,1)S(1)}, u32[]{:S(2)}, u32[]{:S(2)}) %all-to-all-start.1) | async-done | bytes 327712 | tf_op jit(solution)/shard_map/all_to_all | solution.py:331
  100.7 2.5 %finish.1 = bf16[96,1536]{1,0:T(8,128)(2,1)} custom-call(s32[1,1536]{1,0:T(1,128)S(1)} %bitcast.36, bf16[1280,128]{1,0:T(8,128)(2,1)S(1)} %bitcast.31, bf16[96,1536]{1,0:T(8,128)(2,1)S(1)} %residual.1.hidden, s32[1,1536]{1,0:T(1,128)S(1)} %copy-done.2, bf16[96,128]{1,0:T(8,128)(2,1)S(1)} %pad.25.w_out), custom_call_target="tpu_custom_call" | custom-call | tf_op jit(solution)/shard_map/finish/pallas_call | solution.py:455
  (24 shorter events, 0.1 us)
Async XLA Ops:
  0.0 10.6 %copy-start = (bf16[1,96,1536]{2,1,0:T(8,128)(2,1)S(1)}, bf16[1,96,1536]{2,1,0:T(8,128)(2,1)}, u32[]{:S(2)}) copy-start(bf16[1,96,1536]{2,1,0:T(8,128)(2,1)} %param.13) | copy-start | bytes 884740
  1.1 9.5 %copy-start.2 = (s32[1,1536]{1,0:T(1,128)S(1)}, s32[1,1536]{1,0:T(1,128)}, u32[]{:S(2)}) copy-start(s32[1,1536]{1,0:T(1,128)} %mask.5) | copy-start | bytes 18436
  1.1 11.6 %collective-permute-start = (bf16[96,512]{1,0:T(8,128)(2,1)S(1)}, bf16[96,512]{1,0:T(8,128)(2,1)S(1)}, u32[]{:S(2)}, u32[]{:S(2)}) collective-permute-start(bf16[96,512]{1,0:T(8,128)(2,1)S(1)} %get-tuple-element.14), channel_id=1, source_target_pairs={{1,2},{2,1},{3,4},{4,3},{5,6},{6,5},{7,8},{8,7},{9,10},{10,9},{11,... | collective-permute-start | bytes 294920 | tf_op jit(solution)/shard_map/ppermute | solution.py:36
  6.1 4.5 %copy-start.4 = (s32[1,3,8]{2,0,1:T(1,128)S(1)}, s32[1,3,8]{2,0,1:T(1,128)}, u32[]{:S(2)}) copy-start(s32[1,3,8]{2,0,1:T(1,128)} %param.18) | copy-start | bytes 292
  6.1 6.6 %collective-permute-start.1 = (bf16[96,512]{1,0:T(8,128)(2,1)S(1)}, bf16[96,512]{1,0:T(8,128)(2,1)S(1)}, u32[]{:S(2)}, u32[]{:S(2)}) collective-permute-start(bf16[96,512]{1,0:T(8,128)(2,1)S(1)} %get-tuple-element.15), channel_id=1, source_target_pairs={{0,1},{1,0},{2,3},{3,2},{4,5},{5,4},{6,7},{7,6},{8,9},{9,8},{10,11... | collective-permute-start | bytes 294920 | tf_op jit(solution)/shard_map/ppermute | solution.py:36
  10.6 1.1 %copy-start.1 = (bf16[1,27,96,96]{3,2,1,0:T(8,128)(2,1)S(1)}, bf16[1,27,96,96]{3,2,1,0:T(8,128)(2,1)}, u32[]{:S(2)}) copy-start(bf16[1,27,96,96]{3,2,1,0:T(8,128)(2,1)} %param.15) | copy-start | bytes 1492996
  12.7 0.7 copy-start.5
  13.4 5.5 %copy-start.3 = (s32[1,1,1536]{2,1,0:T(1,128)S(1)}, s32[1,1,1536]{2,1,0:T(1,128)}, u32[]{:S(2)}) copy-start(s32[1,1,1536]{2,1,0:T(1,128)} %param.19) | copy-start | bytes 18436
  17.6 3.2 %collective-permute-start.2 = (bf16[192,128]{1,0:T(8,128)(2,1)S(1)}, bf16[192,128]{1,0:T(8,128)(2,1)S(1)}, u32[]{:S(2)}, u32[]{:S(2)}) collective-permute-start(bf16[192,128]{1,0:T(8,128)(2,1)S(1)} %get-tuple-element.20), channel_id=1, source_target_pairs={{0,128},{128,256},{256,384},{1,129},{129,257},{257,385},{2,130},{1... | collective-permute-start | bytes 147464 | tf_op jit(solution)/shard_map/ppermute | solution.py:28
  22.1 23.8 %copy-start.6 = (bf16[1,96,96]{2,1,0:T(8,128)(2,1)S(1)}, bf16[1,96,96]{2,1,0:T(8,128)(2,1)}, u32[]{:S(2)}) copy-start(bf16[1,96,96]{2,1,0:T(8,128)(2,1)} %param.22) | copy-start | bytes 55300
  22.1 38.6 %all-to-all-start = ((bf16[640,2,128]{2,1,0:T(2,128)(2,1)}), bf16[640,2,128]{2,1,0:T(2,128)(2,1)S(1)}, u32[]{:S(2)}, u32[]{:S(2)}) async-start(bf16[640,2,128]{2,1,0:T(2,128)(2,1)} %bitcast.9), calls=%async_computation | async-start | bytes 655360 | tf_op jit(solution)/shard_map/all_to_all | solution.py:331
  45.9 0.7 copy-start.7
  46.6 0.7 copy-start.8
  46.6 1.4 %copy-start.10 = (s32[1,1,1536]{2,1,0:T(1,128)S(1)}, s32[1,1,1536]{2,1,0:T(1,128)}, u32[]{:S(2)}) copy-start(s32[1,1,1536]{2,1,0:T(1,128)} %param.20) | copy-start | bytes 18436
  47.4 0.7 copy-start.11
  68.4 17.6 %copy-start.9 = (bf16[1,96,96]{2,1,0:T(8,128)(2,1)S(1)}, bf16[1,96,96]{2,1,0:T(8,128)(2,1)}, u32[]{:S(2)}) copy-start(bf16[1,96,96]{2,1,0:T(8,128)(2,1)} %param.25) | copy-start | bytes 55300
  68.4 32.3 %all-to-all-start.1 = ((bf16[640,2,128]{2,1,0:T(2,128)(2,1)}), bf16[640,2,128]{2,1,0:T(2,128)(2,1)S(1)}, u32[]{:S(2)}, u32[]{:S(2)}) async-start(bf16[640,2,128]{2,1,0:T(2,128)(2,1)} %bitcast.14), calls=%async_computation.1 | async-start | bytes 655360 | tf_op jit(solution)/shard_map/all_to_all | solution.py:331

commit v4 on v3

--- a/solution.py
+++ b/solution.py
@@ -20,6 +20,7 @@
 CONTRACT_LAST = (((1,), (1,)), ((), ()))
 VMEM_LIMIT = 24 << 20
 FIRST_PEER = 80
+RING = 16
 
 
 def shifted(block, axis, distance):
@@ -58,9 +59,10 @@
         dst[pl.ds(write_index(i), 1), :] = src[i : i + 1, :]
 
 
-def sent_token(order, first, peers):
-    pair = order.shape[1] // peers
-    return lambda i: order[0, (i % peers + first) % peers * pair + i // peers]
+def sent_token(order, peers):
+    count = len(peers)
+    pair = order.shape[1] // count
+    return lambda i: order[0, peers[i % count] * pair + i // count]
 
 
 def pack_rows(slots, packed, with_mask):
@@ -117,7 +119,9 @@
         out[...] = (block[:, here].astype(jnp.float32) * shown).astype(jnp.bfloat16)
 
 
-def layout_kernel(octants, feats, mask, taps, table, weights):
+def layout_kernel(octants, feats, mask, source, table, weights, taps, ready):
+    copy = pltpu.make_async_copy(source, taps, ready)
+    copy.start()
     tokens = feats.shape[1]
     flags = mask[...].astype(jnp.float32)
     values = feats[...].astype(jnp.float32) * flags
@@ -133,12 +137,18 @@
     tail = jnp.where(row == 0, flags, jnp.where(row == 1, child, 0.0))
     table[...] = jnp.concatenate([values, tail], axis=0).T
     weights[...] = jnp.zeros(weights.shape, jnp.bfloat16)
+    copy.wait()
     for k in range(27):
         at = (k % 9) * LANES
-        weights[k // 9, 0:96, at : at + 96] = taps[k]
-
-
-def conv_kernel(rules, own, across, inside, weights, joined, pooled, table, padded, views, halves):
+        down = (k // 9) * LANES
+        weights[down : down + 96, at : at + 96] = taps[k]
+
+
+def conv_kernel(
+    source, own, across, inside, weights, joined, pooled, table, padded, views, halves, rules, ready
+):
+    copy = pltpu.make_async_copy(source, rules, ready)
+    copy.start()
     blocks = own.shape[0] // VOX
     pad_lanes = jnp.zeros((LANES - 96, VOX), jnp.float32)
     for b in range(blocks):
@@ -148,6 +158,8 @@
         values = jnp.concatenate([ref[...].astype(jnp.float32), pad_lanes], axis=0).T
         table[spot] = values.reshape(EDGE, EDGE, EDGE, LANES)
     table[blocks + 2] = jnp.zeros((EDGE, EDGE, EDGE, LANES), jnp.float32)
+
+    copy.wait()
 
     def span(direction):
         if direction < 0:
@@ -186,14 +198,19 @@
                 views[:, k * LANES : (k + 1) * LANES] = window.reshape(
                     (EDGE + 2) * EDGE * EDGE, LANES
                 ).astype(jnp.bfloat16)
-        total = jnp.zeros((VOX, LANES), jnp.float32)
-        for dx in range(3):
-            total = total + lax.dot_general(
-                views[dx * 64 : dx * 64 + VOX, :],
-                weights[dx],
-                CONTRACT_LAST,
-                preferred_element_type=jnp.float32,
-            )
+        first = lax.dot_general(
+            views[0 : VOX + 64, :],
+            weights[0 : 2 * LANES, :],
+            CONTRACT_LAST,
+            preferred_element_type=jnp.float32,
+        )
+        third = lax.dot_general(
+            views[128 : VOX + 128, :],
+            weights[2 * LANES :, :],
+            CONTRACT_LAST,
+            preferred_element_type=jnp.float32,
+        )
+        total = first[:VOX, :LANES] + first[64:, LANES:] + third
         rows = own[b * VOX : (b + 1) * VOX, :]
         conv = total * rows[:, 96:97]
         joined[b * VOX : (b + 1) * VOX, :] = rows + conv
@@ -217,8 +234,8 @@
     return rows + jnp.dot(chosen, below, preferred_element_type=jnp.float32)
 
 
-def gather_kernel(first, peers, order, joined, slots, chosen):
-    gather_rows(sent_token(order, first, peers), joined, slots)
+def gather_kernel(peers, order, joined, slots, chosen):
+    gather_rows(sent_token(order, peers), joined, slots)
     chosen[...] = child_matrix(slots[...])
 
 
@@ -298,10 +315,10 @@
     outbound[...] = packed[...].astype(jnp.bfloat16)
 
 
-def finish_kernel(first, peers, order, returned, hidden, mask, w_out, result, packed, slots, rows):
+def finish_kernel(peers, order, returned, hidden, mask, w_out, result, packed, slots, rows):
     packed[...] = returned[...].astype(jnp.float32)
     unpack_rows(packed, slots, False)
-    scatter_rows(sent_token(order, first, peers), slots, rows)
+    scatter_rows(sent_token(order, peers), slots, rows)
     projected = lax.dot_general(
         w_out[...],
         rows[...].astype(jnp.bfloat16),
@@ -324,12 +341,21 @@
     )
 
 
-def exchange(packed, first):
-    spaces = lax.axis_size("space")
+def peer_order(spaces):
+    first = FIRST_PEER % spaces
+
+    def distance(i):
+        y, z = i // (RING * 2), i // 2 % RING
+        columns = max(spaces // (RING * 2), 1)
+        return min(y, columns - y) + min(z, RING - z)
+
+    return [first] + sorted(set(range(spaces)) - {first}, key=lambda i: (distance(i), i))
+
+
+def exchange(packed, peers):
     tiles = packed.reshape(packed.shape[0] // 2, 2, LANES)
-    peers = [[(first + i) % spaces for i in range(spaces)]]
     return lax.all_to_all(
-        tiles, "space", split_axis=0, concat_axis=0, axis_index_groups=peers, tiled=True
+        tiles, "space", split_axis=0, concat_axis=0, axis_index_groups=[peers], tiled=True
     ).reshape(packed.shape)
 
 
@@ -376,33 +402,39 @@
         layout_kernel,
         (
             jax.ShapeDtypeStruct((tokens, LANES), f32),
-            jax.ShapeDtypeStruct((3, LANES, 9 * LANES), bf16),
+            jax.ShapeDtypeStruct((3 * LANES, 9 * LANES), bf16),
         ),
-        [smem()] + [vmem()] * 3,
+        [smem()] + [vmem()] * 2 + [pl.BlockSpec(memory_space=pltpu.HBM)],
+        [pltpu.VMEM((27, 96, 96), bf16), pltpu.SemaphoreType.DMA],
         name="layout",
-    )(pool_map.reshape(blocks, 1, 8), feats[0], mask, conv_w[0])
+    )(pool_map.reshape(blocks, 1, 8), feats[0], mask, in_hbm(conv_w[0]))
     joined, pooled = call(
         conv_kernel,
         (
             jax.ShapeDtypeStruct((tokens, LANES), f32),
             jax.ShapeDtypeStruct((blocks * 64, LANES), bf16),
         ),
-        [smem()] + [vmem()] * 4,
+        [pl.BlockSpec(memory_space=pltpu.HBM)] + [vmem()] * 4,
         [
             pltpu.VMEM((blocks + 3, EDGE, EDGE, EDGE, LANES), f32),
             pltpu.VMEM((3, EDGE + 2, EDGE + 2, EDGE, LANES), f32),
             pltpu.VMEM(((EDGE + 2) * EDGE * EDGE, 9 * LANES), bf16),
             pltpu.VMEM((16 * EDGE, LANES), f32),
+            pltpu.SMEM((blocks, 1, 26), jnp.int32),
+            pltpu.SemaphoreType.DMA,
         ],
         name="conv",
-    )(rules.reshape(blocks, 1, 26), table, across, inside, weights)
+    )(in_hbm(rules.reshape(blocks, 1, 26)), table, across, inside, weights)
     coarser = shifted(pooled, "section", 1)
-    first = FIRST_PEER % spaces
+    peers = peer_order(spaces)
     order_out = send_order.reshape(1, tokens)
     held = patch_order.reshape(1, tokens)
-    order_in = (held % pair) * spaces + (held // pair + (spaces - first)) % spaces
+    place = jnp.asarray([[peers.index(i) for i in range(spaces)]], bf16)
+    match = (jnp.arange(spaces, dtype=jnp.int32)[:, None] == held // pair).astype(bf16)
+    place = jnp.dot(place, match, preferred_element_type=f32).astype(jnp.int32)
+    order_in = (held % pair) * spaces + place
     slots, chosen = call(
-        functools.partial(gather_kernel, first, spaces),
+        functools.partial(gather_kernel, peers),
         (
             jax.ShapeDtypeStruct((tokens, LANES), f32),
             jax.ShapeDtypeStruct((tokens, 2 * LANES), bf16),
@@ -423,7 +455,7 @@
         [vmem()] * 2,
         name="residual",
     )(joined, coarser)[0]
-    inbound = exchange(message, first)
+    inbound = exchange(message, peers)
 
     def square(weight):
         return jnp.pad(weight[0], ((0, LANES - 96), (0, LANES - 96)))
@@ -451,9 +483,9 @@
         square(w_key),
         square(w_value),
     )[0]
-    returned = exchange(outbound, first)
+    returned = exchange(outbound, peers)
     result = call(
-        functools.partial(finish_kernel, first, spaces),
+        functools.partial(finish_kernel, peers),
         (jax.ShapeDtypeStruct((96, tokens), bf16),),
         [smem()] + [vmem()] * 4,
         [

time: 104 us -> 102 us (0.981)
  starting transfers between devices: 52.1 us -> 50.9 us
  waiting for transfers between devices: 26.7 us -> 25.6 us
    all_to_all x2, starting transfers between devices: 41.4 us -> 40.2 us  [exchange(): lax.all_to_all(tiles, 'space', split_axis=0, concat_axis=0, axis_index_gr...]
    all_to_all x2, waiting for transfers between devices: 26.7 us -> 25.6 us  [exchange(): lax.all_to_all(tiles, 'space', split_axis=0, concat_axis=0, axis_index_gr...]
    unnamed x24 -> x22, local copies, waits for them, and re-layouts: 3.87 us -> 3.46 us
  transfers between devices with their start and end apart: 5 -> 5, of which waited for: 2 -> 2; matrix products, arithmetic and copies ran while one was open for 0% -> 0% of each run, Pallas kernels for 3% -> 4%
where the time goes in v4:
time: 102 us; the launch traced here: 101 us
  starting transfers between devices  50.9 us (50%)
  waiting for transfers between devices  25.6 us (25%)
  Pallas kernels  20.2 us (20%)
  local copies, waits for them, and re-layouts  3.5 us (3%)
    all_to_all x2, starting transfers between devices, exchange(): lax.all_to_all(tiles, 'space', split_axis=0, concat_axis=0, axis_index_gr...  40.2 us
    all_to_all x2, waiting for transfers between devices, exchange(): lax.all_to_all(tiles, 'space', split_axis=0, concat_axis=0, axis_index_gr...  25.6 us
    ppermute x2, starting transfers between devices, swapped(): return lax.ppermute(block, axis, route)  9.41 us
    pallas_call x1, Pallas kernels, shards(): call(attend_kernel, (jax.ShapeDtypeStruct((packed_rows, LANES), bf16),),...  7.76 us
    unnamed x22, local copies, waits for them, and re-layouts  3.46 us
    pallas_call x1, Pallas kernels, shards(): call(conv_kernel, (jax.ShapeDtypeStruct((tokens, LANES), f32), jax.ShapeD...  3.34 us
    pallas_call x1, Pallas kernels, shards(): call(functools.partial(finish_kernel, peers), (jax.ShapeDtypeStruct((96,...  2.51 us
  transfers between devices with their start and end apart: 5, of which 2 were waited for; matrix products, arithmetic and copies ran while one was open for 0% of the time, Pallas kernels for 4%

profile of v4, /device:TPU:1, one launch (start us, length us, event | category | flops | bytes accessed | tf_op | source)
XLA Modules:
  0.0 100.8 jit_solution(4636049096749304231)
XLA Ops:
  0.0 1.1 %send.1 = (bf16[96,512]{1,0:T(8,128)(2,1)S(1)}, bf16[96,512]{1,0:T(8,128)(2,1)S(1)}) custom-call(s32[1,2]{1,0:T(1,128)} %bitcast.30, bf16[96,1536]{1,0:T(8,128)(2,1)} %bitcast.19, s32[1,1536]{1,0:T(1,128)} %mask.5), custom_call_target="tpu_custom_call" | custom-call | tf_op jit(solution)/shard_map/send/pallas_call | solution.py:387
  1.1 0.0 copy-start.1
  1.1 4.9 %collective-permute-start = (bf16[96,512]{1,0:T(8,128)(2,1)S(1)}, bf16[96,512]{1,0:T(8,128)(2,1)S(1)}, u32[]{:S(2)}, u32[]{:S(2)}) collective-permute-start(bf16[96,512]{1,0:T(8,128)(2,1)S(1)} %get-tuple-element.14), channel_id=1, source_target_pairs={{1,2},{2,1},{3,4},{4,3},{5,6},{6,5},{7,8},{8,7},{9,10},{10,9},{11,... | collective-permute-start | bytes 294920 | tf_op jit(solution)/shard_map/ppermute | solution.py:37
  6.1 4.5 %collective-permute-start.1 = (bf16[96,512]{1,0:T(8,128)(2,1)S(1)}, bf16[96,512]{1,0:T(8,128)(2,1)S(1)}, u32[]{:S(2)}, u32[]{:S(2)}) collective-permute-start(bf16[96,512]{1,0:T(8,128)(2,1)S(1)} %get-tuple-element.15), channel_id=1, source_target_pairs={{0,1},{1,0},{2,3},{3,2},{4,5},{5,4},{6,7},{7,6},{8,9},{9,8},{10,11... | collective-permute-start | bytes 294920 | tf_op jit(solution)/shard_map/ppermute | solution.py:37
  10.6 1.8 %layout.1 = (f32[1536,128]{1,0:T(8,128)S(1)}, bf16[384,1152]{1,0:T(8,128)(2,1)S(1)}) custom-call(s32[3,1,8]{2,1,0:T(1,128)S(1)} %bitcast.23, bf16[96,1536]{1,0:T(8,128)(2,1)S(1)} %bitcast.20, s32[1,1536]{1,0:T(1,128)S(1)} %copy-done.1, bf16[27,96,96]{2,1,0:T(8,128)(2,1)} %bitcast.24), custom_call_target="tpu_custom_call" | custom-call | tf_op jit(solution)/shard_map/layout/pallas_call | solution.py:401
  12.4 3.3 %conv.1 = (f32[1536,128]{1,0:T(8,128)S(1)}, bf16[192,128]{1,0:T(8,128)(2,1)S(1)}) custom-call(s32[3,1,26]{2,1,0:T(1,128)} %bitcast.29, f32[1536,128]{1,0:T(8,128)S(1)} %get-tuple-element.13.own, bf16[96,512]{1,0:T(8,128)(2,1)S(1)} %collective-permute-done.across, bf16[96,512]{1,0:T(8,128)(2,1)S(1)} %collective-permute-done.1.inside, ...), custom_call_target="tpu_custom_call" | custom-call | tf_op jit(solution)/shard_map/conv/pallas_call | solution.py:411
  15.8 1.3 %collective-permute-start.2 = (bf16[192,128]{1,0:T(8,128)(2,1)S(1)}, bf16[192,128]{1,0:T(8,128)(2,1)S(1)}, u32[]{:S(2)}, u32[]{:S(2)}) collective-permute-start(bf16[192,128]{1,0:T(8,128)(2,1)S(1)} %get-tuple-element.20), channel_id=1, source_target_pairs={{0,128},{128,256},{256,384},{1,129},{129,257},{257,385},{2,130},{1... | collective-permute-start | bytes 147464 | tf_op jit(solution)/shard_map/ppermute | solution.py:29
  17.1 1.9 %gather.1 = (f32[1536,128]{1,0:T(8,128)S(1)}, bf16[1536,256]{1,0:T(8,128)(2,1)S(1)}) custom-call(s32[1,1536]{1,0:T(1,128)S(1)} %bitcast.21, f32[1536,128]{1,0:T(8,128)S(1)} %get-tuple-element.17.joined), custom_call_target="tpu_custom_call" | custom-call | tf_op jit(solution)/shard_map/gather/pallas_call | solution.py:436
  18.9 1.3 %join.1 = bf16[1280,128]{1,0:T(8,128)(2,1)} custom-call(f32[1536,128]{1,0:T(8,128)S(1)} %get-tuple-element.18.slots, bf16[1536,256]{1,0:T(8,128)(2,1)S(1)} %get-tuple-element.19.chosen, bf16[192,128]{1,0:T(8,128)(2,1)S(1)} %collective-permute-done.2.coarser), custom_call_target="tpu_custom_call" | custom-call | tf_op jit(solution)/shard_map/join/pallas_call | solution.py:445
  20.3 23.6 %all-to-all-start = ((bf16[640,2,128]{2,1,0:T(2,128)(2,1)}), bf16[640,2,128]{2,1,0:T(2,128)(2,1)S(1)}, u32[]{:S(2)}, u32[]{:S(2)}) async-start(bf16[640,2,128]{2,1,0:T(2,128)(2,1)} %bitcast.7), calls=%async_computation | async-start | bytes 655360 | tf_op jit(solution)/shard_map/all_to_all | solution.py:357
  43.9 0.1 divide_reduce_fusion
  44.0 0.0 copy-start.10
  44.0 0.6 copy-done.10
  44.6 0.2 convolution_reduce_fusion
  44.9 0.7 copy-done.4
  45.6 0.7 copy-done.5
  46.4 0.7 copy-done.6
  47.1 0.6 copy-done.9
  47.7 11.1 %all-to-all-done = bf16[640,2,128]{2,1,0:T(2,128)(2,1)S(1)} async-done(((bf16[640,2,128]{2,1,0:T(2,128)(2,1)}), bf16[640,2,128]{2,1,0:T(2,128)(2,1)S(1)}, u32[]{:S(2)}, u32[]{:S(2)}) %all-to-all-start) | async-done | bytes 327712 | tf_op jit(solution)/shard_map/all_to_all | solution.py:357
  58.9 7.8 %attend.1 = bf16[1280,128]{1,0:T(8,128)(2,1)} custom-call(s32[1,1536]{1,0:T(1,128)S(1)} %add.30.order, bf16[1280,128]{1,0:T(8,128)(2,1)S(1)} %bitcast.17, f32[1,128]{1,0:T(1,128)S(1)} %pad_convert_fusion.gain, bf16[128,128]{1,0:T(8,128)(2,1)S(1)} %pad.22.w_query, bf16[128,128]{1,0:T(8,128)(2,1)S(1)} %pad.23.w_key, bf16[128,128]{1,0:T(8,128)(2,1)S(1)} %pad.24.w_value), custom_call_target="tpu_custom_call" | custom-call | tf_op jit(solution)/shard_map/attend/pallas_call | solution.py:463
  66.6 16.6 %all-to-all-start.1 = ((bf16[640,2,128]{2,1,0:T(2,128)(2,1)}), bf16[640,2,128]{2,1,0:T(2,128)(2,1)S(1)}, u32[]{:S(2)}, u32[]{:S(2)}) async-start(bf16[640,2,128]{2,1,0:T(2,128)(2,1)} %bitcast.12), calls=%async_computation.1 | async-start | bytes 655360 | tf_op jit(solution)/shard_map/all_to_all | solution.py:357
  83.3 0.5 residual.1.hidden
  83.8 14.5 %all-to-all-done.1 = bf16[640,2,128]{2,1,0:T(2,128)(2,1)S(1)} async-done(((bf16[640,2,128]{2,1,0:T(2,128)(2,1)}), bf16[640,2,128]{2,1,0:T(2,128)(2,1)S(1)}, u32[]{:S(2)}, u32[]{:S(2)}) %all-to-all-start.1) | async-done | bytes 327712 | tf_op jit(solution)/shard_map/all_to_all | solution.py:357
  98.3 2.5 %finish.1 = bf16[96,1536]{1,0:T(8,128)(2,1)} custom-call(s32[1,1536]{1,0:T(1,128)S(1)} %bitcast.22, bf16[1280,128]{1,0:T(8,128)(2,1)S(1)} %bitcast.18, bf16[96,1536]{1,0:T(8,128)(2,1)S(1)} %residual.1.hidden, s32[1,1536]{1,0:T(1,128)S(1)} %copy-done.1, bf16[96,128]{1,0:T(8,128)(2,1)S(1)} %pad.25.w_out), custom_call_target="tpu_custom_call" | custom-call | tf_op jit(solution)/shard_map/finish/pallas_call | solution.py:487
  (27 shorter events, 0.1 us)
Async XLA Ops:
  0.0 10.6 %copy-start = (bf16[1,96,1536]{2,1,0:T(8,128)(2,1)S(1)}, bf16[1,96,1536]{2,1,0:T(8,128)(2,1)}, u32[]{:S(2)}) copy-start(bf16[1,96,1536]{2,1,0:T(8,128)(2,1)} %param.14) | copy-start | bytes 884740
  1.1 9.5 %copy-start.1 = (s32[1,1536]{1,0:T(1,128)S(1)}, s32[1,1536]{1,0:T(1,128)}, u32[]{:S(2)}) copy-start(s32[1,1536]{1,0:T(1,128)} %mask.5) | copy-start | bytes 18436
  1.1 11.3 %collective-permute-start = (bf16[96,512]{1,0:T(8,128)(2,1)S(1)}, bf16[96,512]{1,0:T(8,128)(2,1)S(1)}, u32[]{:S(2)}, u32[]{:S(2)}) collective-permute-start(bf16[96,512]{1,0:T(8,128)(2,1)S(1)} %get-tuple-element.14), channel_id=1, source_target_pairs={{1,2},{2,1},{3,4},{4,3},{5,6},{6,5},{7,8},{8,7},{9,10},{10,9},{11,... | collective-permute-start | bytes 294920 | tf_op jit(solution)/shard_map/ppermute | solution.py:37
  6.1 4.5 %copy-start.3 = (s32[1,3,8]{2,0,1:T(1,128)S(1)}, s32[1,3,8]{2,0,1:T(1,128)}, u32[]{:S(2)}) copy-start(s32[1,3,8]{2,0,1:T(1,128)} %param.19) | copy-start | bytes 292
  6.1 6.3 %collective-permute-start.1 = (bf16[96,512]{1,0:T(8,128)(2,1)S(1)}, bf16[96,512]{1,0:T(8,128)(2,1)S(1)}, u32[]{:S(2)}, u32[]{:S(2)}) collective-permute-start(bf16[96,512]{1,0:T(8,128)(2,1)S(1)} %get-tuple-element.15), channel_id=1, source_target_pairs={{0,1},{1,0},{2,3},{3,2},{4,5},{5,4},{6,7},{7,6},{8,9},{9,8},{10,11... | collective-permute-start | bytes 294920 | tf_op jit(solution)/shard_map/ppermute | solution.py:37
  12.4 4.7 %copy-start.2 = (s32[1,1,1536]{2,1,0:T(1,128)S(1)}, s32[1,1,1536]{2,1,0:T(1,128)}, u32[]{:S(2)}) copy-start(s32[1,1,1536]{2,1,0:T(1,128)} %param.20) | copy-start | bytes 18436
  15.8 3.2 %collective-permute-start.2 = (bf16[192,128]{1,0:T(8,128)(2,1)S(1)}, bf16[192,128]{1,0:T(8,128)(2,1)S(1)}, u32[]{:S(2)}, u32[]{:S(2)}) collective-permute-start(bf16[192,128]{1,0:T(8,128)(2,1)S(1)} %get-tuple-element.20), channel_id=1, source_target_pairs={{0,128},{128,256},{256,384},{1,129},{129,257},{257,385},{2,130},{1... | collective-permute-start | bytes 147464 | tf_op jit(solution)/shard_map/ppermute | solution.py:29
  20.3 23.6 %copy-start.8 = (s32[1,1,1536]{2,1,0:T(1,128)S(1)}, s32[1,1,1536]{2,1,0:T(1,128)}, u32[]{:S(2)}) copy-start(s32[1,1,1536]{2,1,0:T(1,128)} %param.21) | copy-start | bytes 18436
  20.3 38.6 %all-to-all-start = ((bf16[640,2,128]{2,1,0:T(2,128)(2,1)}), bf16[640,2,128]{2,1,0:T(2,128)(2,1)S(1)}, u32[]{:S(2)}, u32[]{:S(2)}) async-start(bf16[640,2,128]{2,1,0:T(2,128)(2,1)} %bitcast.7), calls=%async_computation | async-start | bytes 655360 | tf_op jit(solution)/shard_map/all_to_all | solution.py:357
  44.0 0.7 copy-start.10
  44.9 0.7 copy-start.4
  45.6 0.7 copy-start.5
  46.3 0.7 copy-start.6
  47.1 0.7 copy-start.9
  66.6 16.6 %copy-start.7 = (bf16[1,96,96]{2,1,0:T(8,128)(2,1)S(1)}, bf16[1,96,96]{2,1,0:T(8,128)(2,1)}, u32[]{:S(2)}) copy-start(bf16[1,96,96]{2,1,0:T(8,128)(2,1)} %param.26) | copy-start | bytes 55300
  66.6 31.6 %all-to-all-start.1 = ((bf16[640,2,128]{2,1,0:T(2,128)(2,1)}), bf16[640,2,128]{2,1,0:T(2,128)(2,1)S(1)}, u32[]{:S(2)}, u32[]{:S(2)}) async-start(bf16[640,2,128]{2,1,0:T(2,128)(2,1)} %bitcast.12), calls=%async_computation.1 | async-start | bytes 655360 | tf_op jit(solution)/shard_map/all_to_all | solution.py:357

commit v5 on v4

--- a/solution.py
+++ b/solution.py
@@ -103,13 +103,17 @@
             slots[t * peers : (t + 1) * peers, :] = value
 
 
-def send_kernel(lists, feats, mask, across, inside, slots, block, flags, ready):
+def send_kernel(
+    lists, feats, mask, source, across, inside, taps, slots, block, flags, ready, later
+):
     copies = [
         pltpu.make_async_copy(source, target, ready.at[i])
         for i, (source, target) in enumerate(((lists, slots), (feats, block), (mask, flags)))
     ]
+    behind = pltpu.make_async_copy(source, taps, later)
     for copy in copies:
         copy.start()
+    behind.start()
     for copy in copies:
         copy.wait()
     odd = lax.rem(lax.axis_index("space"), 2)
@@ -117,11 +121,10 @@
         here = pl.ds(pl.multiple_of(slots[0, row_index] * VOX, VOX), VOX)
         shown = flags[:, here].astype(jnp.float32)
         out[...] = (block[:, here].astype(jnp.float32) * shown).astype(jnp.bfloat16)
-
-
-def layout_kernel(octants, feats, mask, source, table, weights, taps, ready):
-    copy = pltpu.make_async_copy(source, taps, ready)
-    copy.start()
+    behind.wait()
+
+
+def layout_kernel(octants, feats, mask, taps, table, weights):
     tokens = feats.shape[1]
     flags = mask[...].astype(jnp.float32)
     values = feats[...].astype(jnp.float32) * flags
@@ -137,7 +140,6 @@
     tail = jnp.where(row == 0, flags, jnp.where(row == 1, child, 0.0))
     table[...] = jnp.concatenate([values, tail], axis=0).T
     weights[...] = jnp.zeros(weights.shape, jnp.bfloat16)
-    copy.wait()
     for k in range(27):
         at = (k % 9) * LANES
         down = (k // 9) * LANES
@@ -384,18 +386,19 @@
     def in_hbm(array):
         return pltpu.with_memory_space_constraint(array, pltpu.HBM)
 
-    across, inside = call(
+    across, inside, taps = call(
         send_kernel,
-        (jax.ShapeDtypeStruct((96, VOX), bf16),) * 2,
-        [pl.BlockSpec(memory_space=pltpu.HBM)] * 3,
+        (jax.ShapeDtypeStruct((96, VOX), bf16),) * 2 + (jax.ShapeDtypeStruct((27, 96, 96), bf16),),
+        [pl.BlockSpec(memory_space=pltpu.HBM)] * 4,
         [
             pltpu.SMEM((1, 2), jnp.int32),
             pltpu.VMEM((96, tokens), bf16),
             pltpu.VMEM((1, tokens), jnp.int32),
             pltpu.SemaphoreType.DMA((3,)),
+            pltpu.SemaphoreType.DMA,
         ],
         name="send",
-    )(in_hbm(send_lists.reshape(1, 2)), in_hbm(feats[0]), in_hbm(mask))
+    )(in_hbm(send_lists.reshape(1, 2)), in_hbm(feats[0]), in_hbm(mask), in_hbm(conv_w[0]))
     across = swapped(across, "space", 1)
     inside = swapped(inside, "space", 0)
     table, weights = call(
@@ -404,10 +407,9 @@
             jax.ShapeDtypeStruct((tokens, LANES), f32),
             jax.ShapeDtypeStruct((3 * LANES, 9 * LANES), bf16),
         ),
-        [smem()] + [vmem()] * 2 + [pl.BlockSpec(memory_space=pltpu.HBM)],
-        [pltpu.VMEM((27, 96, 96), bf16), pltpu.SemaphoreType.DMA],
+        [smem()] + [vmem()] * 3,
         name="layout",
-    )(pool_map.reshape(blocks, 1, 8), feats[0], mask, in_hbm(conv_w[0]))
+    )(pool_map.reshape(blocks, 1, 8), feats[0], mask, taps)
     joined, pooled = call(
         conv_kernel,
         (

time: 102 us -> 101 us (level)
  transfers between devices with their start and end apart: 5 -> 5, of which waited for: 2 -> 2; matrix products, arithmetic and copies ran while one was open for 0% -> 0% of each run, Pallas kernels for 4% -> 3%
where the time goes in v5:
time: 101 us; the launch traced here: 100 us
  starting transfers between devices  51.1 us (51%)
  waiting for transfers between devices  25.6 us (25%)
  Pallas kernels  19.6 us (19%)
  local copies, waits for them, and re-layouts  3.5 us (3%)
    all_to_all x2, starting transfers between devices, exchange(): lax.all_to_all(tiles, 'space', split_axis=0, concat_axis=0, axis_index_gr...  40.4 us
    all_to_all x2, waiting for transfers between devices, exchange(): lax.all_to_all(tiles, 'space', split_axis=0, concat_axis=0, axis_index_gr...  25.6 us
    ppermute x2, starting transfers between devices, swapped(): return lax.ppermute(block, axis, route)  9.41 us
    pallas_call x1, Pallas kernels, shards(): call(attend_kernel, (jax.ShapeDtypeStruct((packed_rows, LANES), bf16),),...  7.77 us
    unnamed x22, local copies, waits for them, and re-layouts  3.46 us
    pallas_call x1, Pallas kernels, shards(): call(conv_kernel, (jax.ShapeDtypeStruct((tokens, LANES), f32), jax.ShapeD...  3.37 us
    pallas_call x1, Pallas kernels, shards(): call(functools.partial(finish_kernel, peers), (jax.ShapeDtypeStruct((96,...  2.51 us
  transfers between devices with their start and end apart: 5, of which 2 were waited for; matrix products, arithmetic and copies ran while one was open for 0% of the time, Pallas kernels for 3%

profile of v5, /device:TPU:1, one launch (start us, length us, event | category | flops | bytes accessed | tf_op | source)
XLA Modules:
  0.0 100.4 jit_solution(7049838495421870256)
XLA Ops:
  0.0 1.3 %send.1 = (bf16[96,512]{1,0:T(8,128)(2,1)S(1)}, bf16[96,512]{1,0:T(8,128)(2,1)S(1)}, bf16[27,96,96]{2,1,0:T(8,128)(2,1)S(1)}) custom-call(s32[1,2]{1,0:T(1,128)} %bitcast.30, bf16[96,1536]{1,0:T(8,128)(2,1)} %bitcast.19, s32[1,1536]{1,0:T(1,128)} %mask.5, bf16[27,96,96]{2,1,0:T(8,128)(2,1)} %bitcast.24), custom_call_target="tpu_custom_call" | custom-call | tf_op jit(solution)/shard_map/send/pallas_call | solution.py:389
  1.3 4.9 %collective-permute-start = (bf16[96,512]{1,0:T(8,128)(2,1)S(1)}, bf16[96,512]{1,0:T(8,128)(2,1)S(1)}, u32[]{:S(2)}, u32[]{:S(2)}) collective-permute-start(bf16[96,512]{1,0:T(8,128)(2,1)S(1)} %get-tuple-element.16), channel_id=1, source_target_pairs={{1,2},{2,1},{3,4},{4,3},{5,6},{6,5},{7,8},{8,7},{9,10},{10,9},{11,... | collective-permute-start | bytes 294920 | tf_op jit(solution)/shard_map/ppermute | solution.py:37
  6.2 0.0 copy-start.3
  6.2 4.5 %collective-permute-start.1 = (bf16[96,512]{1,0:T(8,128)(2,1)S(1)}, bf16[96,512]{1,0:T(8,128)(2,1)S(1)}, u32[]{:S(2)}, u32[]{:S(2)}) collective-permute-start(bf16[96,512]{1,0:T(8,128)(2,1)S(1)} %get-tuple-element.17), channel_id=1, source_target_pairs={{0,1},{1,0},{2,3},{3,2},{4,5},{5,4},{6,7},{7,6},{8,9},{9,8},{10,11... | collective-permute-start | bytes 294920 | tf_op jit(solution)/shard_map/ppermute | solution.py:37
  10.8 1.0 layout.1
  11.8 3.4 %conv.1 = (f32[1536,128]{1,0:T(8,128)S(1)}, bf16[192,128]{1,0:T(8,128)(2,1)S(1)}) custom-call(s32[3,1,26]{2,1,0:T(1,128)} %bitcast.29, f32[1536,128]{1,0:T(8,128)S(1)} %get-tuple-element.15.own, bf16[96,512]{1,0:T(8,128)(2,1)S(1)} %collective-permute-done.across, bf16[96,512]{1,0:T(8,128)(2,1)S(1)} %collective-permute-done.1.inside, ...), custom_call_target="tpu_custom_call" | custom-call | tf_op jit(solution)/shard_map/conv/pallas_call | solution.py:413
  15.2 1.3 %collective-permute-start.2 = (bf16[192,128]{1,0:T(8,128)(2,1)S(1)}, bf16[192,128]{1,0:T(8,128)(2,1)S(1)}, u32[]{:S(2)}, u32[]{:S(2)}) collective-permute-start(bf16[192,128]{1,0:T(8,128)(2,1)S(1)} %get-tuple-element.22), channel_id=1, source_target_pairs={{0,128},{128,256},{256,384},{1,129},{129,257},{257,385},{2,130},{1... | collective-permute-start | bytes 147464 | tf_op jit(solution)/shard_map/ppermute | solution.py:29
  16.5 1.9 %gather.1 = (f32[1536,128]{1,0:T(8,128)S(1)}, bf16[1536,256]{1,0:T(8,128)(2,1)S(1)}) custom-call(s32[1,1536]{1,0:T(1,128)S(1)} %bitcast.21, f32[1536,128]{1,0:T(8,128)S(1)} %get-tuple-element.19.joined), custom_call_target="tpu_custom_call" | custom-call | tf_op jit(solution)/shard_map/gather/pallas_call | solution.py:438
  18.4 1.3 %join.1 = bf16[1280,128]{1,0:T(8,128)(2,1)} custom-call(f32[1536,128]{1,0:T(8,128)S(1)} %get-tuple-element.20.slots, bf16[1536,256]{1,0:T(8,128)(2,1)S(1)} %get-tuple-element.21.chosen, bf16[192,128]{1,0:T(8,128)(2,1)S(1)} %collective-permute-done.2.coarser), custom_call_target="tpu_custom_call" | custom-call | tf_op jit(solution)/shard_map/join/pallas_call | solution.py:447
  19.7 23.8 %all-to-all-start = ((bf16[640,2,128]{2,1,0:T(2,128)(2,1)}), bf16[640,2,128]{2,1,0:T(2,128)(2,1)S(1)}, u32[]{:S(2)}, u32[]{:S(2)}) async-start(bf16[640,2,128]{2,1,0:T(2,128)(2,1)} %bitcast.7), calls=%async_computation | async-start | bytes 655360 | tf_op jit(solution)/shard_map/all_to_all | solution.py:359
  43.5 0.1 divide_reduce_fusion
  43.6 0.0 copy-start.10
  43.6 0.6 copy-done.10
  44.2 0.2 convolution_reduce_fusion
  44.5 0.7 copy-done.4
  45.2 0.7 copy-done.5
  46.0 0.7 copy-done.6
  46.7 0.6 copy-done.9
  47.4 11.1 %all-to-all-done = bf16[640,2,128]{2,1,0:T(2,128)(2,1)S(1)} async-done(((bf16[640,2,128]{2,1,0:T(2,128)(2,1)}), bf16[640,2,128]{2,1,0:T(2,128)(2,1)S(1)}, u32[]{:S(2)}, u32[]{:S(2)}) %all-to-all-start) | async-done | bytes 327712 | tf_op jit(solution)/shard_map/all_to_all | solution.py:359
  58.5 7.8 %attend.1 = bf16[1280,128]{1,0:T(8,128)(2,1)} custom-call(s32[1,1536]{1,0:T(1,128)S(1)} %add.30.order, bf16[1280,128]{1,0:T(8,128)(2,1)S(1)} %bitcast.17, f32[1,128]{1,0:T(1,128)S(1)} %pad_convert_fusion.gain, bf16[128,128]{1,0:T(8,128)(2,1)S(1)} %pad.22.w_query, bf16[128,128]{1,0:T(8,128)(2,1)S(1)} %pad.23.w_key, bf16[128,128]{1,0:T(8,128)(2,1)S(1)} %pad.24.w_value), custom_call_target="tpu_custom_call" | custom-call | tf_op jit(solution)/shard_map/attend/pallas_call | solution.py:465
  66.3 16.6 %all-to-all-start.1 = ((bf16[640,2,128]{2,1,0:T(2,128)(2,1)}), bf16[640,2,128]{2,1,0:T(2,128)(2,1)S(1)}, u32[]{:S(2)}, u32[]{:S(2)}) async-start(bf16[640,2,128]{2,1,0:T(2,128)(2,1)} %bitcast.12), calls=%async_computation.1 | async-start | bytes 655360 | tf_op jit(solution)/shard_map/all_to_all | solution.py:359
  82.9 0.5 residual.1.hidden
  83.4 14.5 %all-to-all-done.1 = bf16[640,2,128]{2,1,0:T(2,128)(2,1)S(1)} async-done(((bf16[640,2,128]{2,1,0:T(2,128)(2,1)}), bf16[640,2,128]{2,1,0:T(2,128)(2,1)S(1)}, u32[]{:S(2)}, u32[]{:S(2)}) %all-to-all-start.1) | async-done | bytes 327712 | tf_op jit(solution)/shard_map/all_to_all | solution.py:359
  97.9 2.5 %finish.1 = bf16[96,1536]{1,0:T(8,128)(2,1)} custom-call(s32[1,1536]{1,0:T(1,128)S(1)} %bitcast.22, bf16[1280,128]{1,0:T(8,128)(2,1)S(1)} %bitcast.18, bf16[96,1536]{1,0:T(8,128)(2,1)S(1)} %residual.1.hidden, s32[1,1536]{1,0:T(1,128)S(1)} %copy-done.1, bf16[96,128]{1,0:T(8,128)(2,1)S(1)} %pad.25.w_out), custom_call_target="tpu_custom_call" | custom-call | tf_op jit(solution)/shard_map/finish/pallas_call | solution.py:489
  (27 shorter events, 0.1 us)
Async XLA Ops:
  0.0 10.7 %copy-start = (bf16[1,96,1536]{2,1,0:T(8,128)(2,1)S(1)}, bf16[1,96,1536]{2,1,0:T(8,128)(2,1)}, u32[]{:S(2)}) copy-start(bf16[1,96,1536]{2,1,0:T(8,128)(2,1)} %param.14) | copy-start | bytes 884740
  1.3 9.5 %copy-start.1 = (s32[1,1536]{1,0:T(1,128)S(1)}, s32[1,1536]{1,0:T(1,128)}, u32[]{:S(2)}) copy-start(s32[1,1536]{1,0:T(1,128)} %mask.5) | copy-start | bytes 18436
  1.3 10.5 %collective-permute-start = (bf16[96,512]{1,0:T(8,128)(2,1)S(1)}, bf16[96,512]{1,0:T(8,128)(2,1)S(1)}, u32[]{:S(2)}, u32[]{:S(2)}) collective-permute-start(bf16[96,512]{1,0:T(8,128)(2,1)S(1)} %get-tuple-element.16), channel_id=1, source_target_pairs={{1,2},{2,1},{3,4},{4,3},{5,6},{6,5},{7,8},{8,7},{9,10},{10,9},{11,... | collective-permute-start | bytes 294920 | tf_op jit(solution)/shard_map/ppermute | solution.py:37
  6.2 4.5 %copy-start.3 = (s32[1,3,8]{2,0,1:T(1,128)S(1)}, s32[1,3,8]{2,0,1:T(1,128)}, u32[]{:S(2)}) copy-start(s32[1,3,8]{2,0,1:T(1,128)} %param.19) | copy-start | bytes 292
  6.2 5.5 %collective-permute-start.1 = (bf16[96,512]{1,0:T(8,128)(2,1)S(1)}, bf16[96,512]{1,0:T(8,128)(2,1)S(1)}, u32[]{:S(2)}, u32[]{:S(2)}) collective-permute-start(bf16[96,512]{1,0:T(8,128)(2,1)S(1)} %get-tuple-element.17), channel_id=1, source_target_pairs={{0,1},{1,0},{2,3},{3,2},{4,5},{5,4},{6,7},{7,6},{8,9},{9,8},{10,11... | collective-permute-start | bytes 294920 | tf_op jit(solution)/shard_map/ppermute | solution.py:37
  11.8 4.7 %copy-start.2 = (s32[1,1,1536]{2,1,0:T(1,128)S(1)}, s32[1,1,1536]{2,1,0:T(1,128)}, u32[]{:S(2)}) copy-start(s32[1,1,1536]{2,1,0:T(1,128)} %param.20) | copy-start | bytes 18436
  15.2 3.2 %collective-permute-start.2 = (bf16[192,128]{1,0:T(8,128)(2,1)S(1)}, bf16[192,128]{1,0:T(8,128)(2,1)S(1)}, u32[]{:S(2)}, u32[]{:S(2)}) collective-permute-start(bf16[192,128]{1,0:T(8,128)(2,1)S(1)} %get-tuple-element.22), channel_id=1, source_target_pairs={{0,128},{128,256},{256,384},{1,129},{129,257},{257,385},{2,130},{1... | collective-permute-start | bytes 147464 | tf_op jit(solution)/shard_map/ppermute | solution.py:29
  19.7 23.8 %copy-start.8 = (s32[1,1,1536]{2,1,0:T(1,128)S(1)}, s32[1,1,1536]{2,1,0:T(1,128)}, u32[]{:S(2)}) copy-start(s32[1,1,1536]{2,1,0:T(1,128)} %param.21) | copy-start | bytes 18436
  19.7 38.8 %all-to-all-start = ((bf16[640,2,128]{2,1,0:T(2,128)(2,1)}), bf16[640,2,128]{2,1,0:T(2,128)(2,1)S(1)}, u32[]{:S(2)}, u32[]{:S(2)}) async-start(bf16[640,2,128]{2,1,0:T(2,128)(2,1)} %bitcast.7), calls=%async_computation | async-start | bytes 655360 | tf_op jit(solution)/shard_map/all_to_all | solution.py:359
  43.6 0.7 copy-start.10
  44.5 0.7 copy-start.4
  45.2 0.7 copy-start.5
  46.0 0.7 copy-start.6
  46.7 0.7 copy-start.9
  66.3 16.6 %copy-start.7 = (bf16[1,96,96]{2,1,0:T(8,128)(2,1)S(1)}, bf16[1,96,96]{2,1,0:T(8,128)(2,1)}, u32[]{:S(2)}) copy-start(bf16[1,96,96]{2,1,0:T(8,128)(2,1)} %param.26) | copy-start | bytes 55300
  66.3 31.6 %all-to-all-start.1 = ((bf16[640,2,128]{2,1,0:T(2,128)(2,1)}), bf16[640,2,128]{2,1,0:T(2,128)(2,1)S(1)}, u32[]{:S(2)}, u32[]{:S(2)}) async-start(bf16[640,2,128]{2,1,0:T(2,128)(2,1)} %bitcast.12), calls=%async_computation.1 | async-start | bytes 655360 | tf_op jit(solution)/shard_map/all_to_all | solution.py:359

commit v6 on v5

--- a/solution.py
+++ b/solution.py
@@ -19,7 +19,7 @@
 ROWS = 10
 CONTRACT_LAST = (((1,), (1,)), ((), ()))
 VMEM_LIMIT = 24 << 20
-FIRST_PEER = 80
+FIRST_PEER = 112
 RING = 16
 
 

time: 101 us -> 101 us (level)
  no operation moved by 1% of the time
where the time goes in v6:
time: 101 us; the launch traced here: 100 us
  starting transfers between devices  50.2 us (50%)
  waiting for transfers between devices  26.4 us (26%)
  Pallas kernels  19.6 us (19%)
  local copies, waits for them, and re-layouts  3.5 us (3%)
    all_to_all x2, starting transfers between devices, exchange(): lax.all_to_all(tiles, 'space', split_axis=0, concat_axis=0, axis_index_gr...  39.5 us
    all_to_all x2, waiting for transfers between devices, exchange(): lax.all_to_all(tiles, 'space', split_axis=0, concat_axis=0, axis_index_gr...  26.4 us
    ppermute x2, starting transfers between devices, swapped(): return lax.ppermute(block, axis, route)  9.41 us
    pallas_call x1, Pallas kernels, shards(): call(attend_kernel, (jax.ShapeDtypeStruct((packed_rows, LANES), bf16),),...  7.76 us
    unnamed x22, local copies, waits for them, and re-layouts  3.46 us
    pallas_call x1, Pallas kernels, shards(): call(conv_kernel, (jax.ShapeDtypeStruct((tokens, LANES), f32), jax.ShapeD...  3.37 us
    pallas_call x1, Pallas kernels, shards(): call(functools.partial(finish_kernel, peers), (jax.ShapeDtypeStruct((96,...  2.51 us
  transfers between devices with their start and end apart: 5, of which 2 were waited for; matrix products, arithmetic and copies ran while one was open for 0% of the time, Pallas kernels for 3%

profile of v6, /device:TPU:1, one launch (start us, length us, event | category | flops | bytes accessed | tf_op | source)
XLA Modules:
  0.0 100.4 jit_solution(14386789812535311025)
XLA Ops:
  0.0 1.3 %send.1 = (bf16[96,512]{1,0:T(8,128)(2,1)S(1)}, bf16[96,512]{1,0:T(8,128)(2,1)S(1)}, bf16[27,96,96]{2,1,0:T(8,128)(2,1)S(1)}) custom-call(s32[1,2]{1,0:T(1,128)} %bitcast.30, bf16[96,1536]{1,0:T(8,128)(2,1)} %bitcast.19, s32[1,1536]{1,0:T(1,128)} %mask.5, bf16[27,96,96]{2,1,0:T(8,128)(2,1)} %bitcast.24), custom_call_target="tpu_custom_call" | custom-call | tf_op jit(solution)/shard_map/send/pallas_call | solution.py:389
  1.3 0.0 copy-start.1
  1.3 4.9 %collective-permute-start = (bf16[96,512]{1,0:T(8,128)(2,1)S(1)}, bf16[96,512]{1,0:T(8,128)(2,1)S(1)}, u32[]{:S(2)}, u32[]{:S(2)}) collective-permute-start(bf16[96,512]{1,0:T(8,128)(2,1)S(1)} %get-tuple-element.16), channel_id=1, source_target_pairs={{1,2},{2,1},{3,4},{4,3},{5,6},{6,5},{7,8},{8,7},{9,10},{10,9},{11,... | collective-permute-start | bytes 294920 | tf_op jit(solution)/shard_map/ppermute | solution.py:37
  6.2 4.5 %collective-permute-start.1 = (bf16[96,512]{1,0:T(8,128)(2,1)S(1)}, bf16[96,512]{1,0:T(8,128)(2,1)S(1)}, u32[]{:S(2)}, u32[]{:S(2)}) collective-permute-start(bf16[96,512]{1,0:T(8,128)(2,1)S(1)} %get-tuple-element.17), channel_id=1, source_target_pairs={{0,1},{1,0},{2,3},{3,2},{4,5},{5,4},{6,7},{7,6},{8,9},{9,8},{10,11... | collective-permute-start | bytes 294920 | tf_op jit(solution)/shard_map/ppermute | solution.py:37
  10.8 1.0 layout.1
  11.8 3.4 %conv.1 = (f32[1536,128]{1,0:T(8,128)S(1)}, bf16[192,128]{1,0:T(8,128)(2,1)S(1)}) custom-call(s32[3,1,26]{2,1,0:T(1,128)} %bitcast.29, f32[1536,128]{1,0:T(8,128)S(1)} %get-tuple-element.15.own, bf16[96,512]{1,0:T(8,128)(2,1)S(1)} %collective-permute-done.across, bf16[96,512]{1,0:T(8,128)(2,1)S(1)} %collective-permute-done.1.inside, ...), custom_call_target="tpu_custom_call" | custom-call | tf_op jit(solution)/shard_map/conv/pallas_call | solution.py:413
  15.2 1.3 %collective-permute-start.2 = (bf16[192,128]{1,0:T(8,128)(2,1)S(1)}, bf16[192,128]{1,0:T(8,128)(2,1)S(1)}, u32[]{:S(2)}, u32[]{:S(2)}) collective-permute-start(bf16[192,128]{1,0:T(8,128)(2,1)S(1)} %get-tuple-element.22), channel_id=1, source_target_pairs={{0,128},{128,256},{256,384},{1,129},{129,257},{257,385},{2,130},{1... | collective-permute-start | bytes 147464 | tf_op jit(solution)/shard_map/ppermute | solution.py:29
  16.5 1.9 %gather.1 = (f32[1536,128]{1,0:T(8,128)S(1)}, bf16[1536,256]{1,0:T(8,128)(2,1)S(1)}) custom-call(s32[1,1536]{1,0:T(1,128)S(1)} %bitcast.21, f32[1536,128]{1,0:T(8,128)S(1)} %get-tuple-element.19.joined), custom_call_target="tpu_custom_call" | custom-call | tf_op jit(solution)/shard_map/gather/pallas_call | solution.py:438
  18.4 1.3 %join.1 = bf16[1280,128]{1,0:T(8,128)(2,1)} custom-call(f32[1536,128]{1,0:T(8,128)S(1)} %get-tuple-element.20.slots, bf16[1536,256]{1,0:T(8,128)(2,1)S(1)} %get-tuple-element.21.chosen, bf16[192,128]{1,0:T(8,128)(2,1)S(1)} %collective-permute-done.2.coarser), custom_call_target="tpu_custom_call" | custom-call | tf_op jit(solution)/shard_map/join/pallas_call | solution.py:447
  19.7 23.3 %all-to-all-start = ((bf16[640,2,128]{2,1,0:T(2,128)(2,1)}), bf16[640,2,128]{2,1,0:T(2,128)(2,1)S(1)}, u32[]{:S(2)}, u32[]{:S(2)}) async-start(bf16[640,2,128]{2,1,0:T(2,128)(2,1)} %bitcast.7), calls=%async_computation | async-start | bytes 655360 | tf_op jit(solution)/shard_map/all_to_all | solution.py:359
  43.1 0.1 divide_reduce_fusion
  43.1 0.0 copy-start.10
  43.2 0.6 copy-done.10
  43.8 0.2 convolution_reduce_fusion
  44.1 0.7 copy-done.4
  44.8 0.7 copy-done.5
  45.5 0.7 copy-done.6
  46.3 0.6 copy-done.9
  46.9 11.5 %all-to-all-done = bf16[640,2,128]{2,1,0:T(2,128)(2,1)S(1)} async-done(((bf16[640,2,128]{2,1,0:T(2,128)(2,1)}), bf16[640,2,128]{2,1,0:T(2,128)(2,1)S(1)}, u32[]{:S(2)}, u32[]{:S(2)}) %all-to-all-start) | async-done | bytes 327712 | tf_op jit(solution)/shard_map/all_to_all | solution.py:359
  58.5 7.8 %attend.1 = bf16[1280,128]{1,0:T(8,128)(2,1)} custom-call(s32[1,1536]{1,0:T(1,128)S(1)} %add.30.order, bf16[1280,128]{1,0:T(8,128)(2,1)S(1)} %bitcast.17, f32[1,128]{1,0:T(1,128)S(1)} %pad_convert_fusion.gain, bf16[128,128]{1,0:T(8,128)(2,1)S(1)} %pad.22.w_query, bf16[128,128]{1,0:T(8,128)(2,1)S(1)} %pad.23.w_key, bf16[128,128]{1,0:T(8,128)(2,1)S(1)} %pad.24.w_value), custom_call_target="tpu_custom_call" | custom-call | tf_op jit(solution)/shard_map/attend/pallas_call | solution.py:465
  66.2 16.2 %all-to-all-start.1 = ((bf16[640,2,128]{2,1,0:T(2,128)(2,1)}), bf16[640,2,128]{2,1,0:T(2,128)(2,1)S(1)}, u32[]{:S(2)}, u32[]{:S(2)}) async-start(bf16[640,2,128]{2,1,0:T(2,128)(2,1)} %bitcast.12), calls=%async_computation.1 | async-start | bytes 655360 | tf_op jit(solution)/shard_map/all_to_all | solution.py:359
  82.5 0.5 residual.1.hidden
  83.0 14.9 %all-to-all-done.1 = bf16[640,2,128]{2,1,0:T(2,128)(2,1)S(1)} async-done(((bf16[640,2,128]{2,1,0:T(2,128)(2,1)}), bf16[640,2,128]{2,1,0:T(2,128)(2,1)S(1)}, u32[]{:S(2)}, u32[]{:S(2)}) %all-to-all-start.1) | async-done | bytes 327712 | tf_op jit(solution)/shard_map/all_to_all | solution.py:359
  97.9 2.5 %finish.1 = bf16[96,1536]{1,0:T(8,128)(2,1)} custom-call(s32[1,1536]{1,0:T(1,128)S(1)} %bitcast.22, bf16[1280,128]{1,0:T(8,128)(2,1)S(1)} %bitcast.18, bf16[96,1536]{1,0:T(8,128)(2,1)S(1)} %residual.1.hidden, s32[1,1536]{1,0:T(1,128)S(1)} %copy-done.1, bf16[96,128]{1,0:T(8,128)(2,1)S(1)} %pad.25.w_out), custom_call_target="tpu_custom_call" | custom-call | tf_op jit(solution)/shard_map/finish/pallas_call | solution.py:489
  (27 shorter events, 0.1 us)
Async XLA Ops:
  0.0 10.7 %copy-start = (bf16[1,96,1536]{2,1,0:T(8,128)(2,1)S(1)}, bf16[1,96,1536]{2,1,0:T(8,128)(2,1)}, u32[]{:S(2)}) copy-start(bf16[1,96,1536]{2,1,0:T(8,128)(2,1)} %param.14) | copy-start | bytes 884740
  1.3 9.5 %copy-start.1 = (s32[1,1536]{1,0:T(1,128)S(1)}, s32[1,1536]{1,0:T(1,128)}, u32[]{:S(2)}) copy-start(s32[1,1536]{1,0:T(1,128)} %mask.5) | copy-start | bytes 18436
  1.3 10.5 %collective-permute-start = (bf16[96,512]{1,0:T(8,128)(2,1)S(1)}, bf16[96,512]{1,0:T(8,128)(2,1)S(1)}, u32[]{:S(2)}, u32[]{:S(2)}) collective-permute-start(bf16[96,512]{1,0:T(8,128)(2,1)S(1)} %get-tuple-element.16), channel_id=1, source_target_pairs={{1,2},{2,1},{3,4},{4,3},{5,6},{6,5},{7,8},{8,7},{9,10},{10,9},{11,... | collective-permute-start | bytes 294920 | tf_op jit(solution)/shard_map/ppermute | solution.py:37
  6.2 4.5 %copy-start.3 = (s32[1,3,8]{2,0,1:T(1,128)S(1)}, s32[1,3,8]{2,0,1:T(1,128)}, u32[]{:S(2)}) copy-start(s32[1,3,8]{2,0,1:T(1,128)} %param.19) | copy-start | bytes 292
  6.2 5.5 %collective-permute-start.1 = (bf16[96,512]{1,0:T(8,128)(2,1)S(1)}, bf16[96,512]{1,0:T(8,128)(2,1)S(1)}, u32[]{:S(2)}, u32[]{:S(2)}) collective-permute-start(bf16[96,512]{1,0:T(8,128)(2,1)S(1)} %get-tuple-element.17), channel_id=1, source_target_pairs={{0,1},{1,0},{2,3},{3,2},{4,5},{5,4},{6,7},{7,6},{8,9},{9,8},{10,11... | collective-permute-start | bytes 294920 | tf_op jit(solution)/shard_map/ppermute | solution.py:37
  11.8 4.7 %copy-start.2 = (s32[1,1,1536]{2,1,0:T(1,128)S(1)}, s32[1,1,1536]{2,1,0:T(1,128)}, u32[]{:S(2)}) copy-start(s32[1,1,1536]{2,1,0:T(1,128)} %param.20) | copy-start | bytes 18436
  15.2 3.2 %collective-permute-start.2 = (bf16[192,128]{1,0:T(8,128)(2,1)S(1)}, bf16[192,128]{1,0:T(8,128)(2,1)S(1)}, u32[]{:S(2)}, u32[]{:S(2)}) collective-permute-start(bf16[192,128]{1,0:T(8,128)(2,1)S(1)} %get-tuple-element.22), channel_id=1, source_target_pairs={{0,128},{128,256},{256,384},{1,129},{129,257},{257,385},{2,130},{1... | collective-permute-start | bytes 147464 | tf_op jit(solution)/shard_map/ppermute | solution.py:29
  19.7 23.3 %copy-start.8 = (s32[1,1,1536]{2,1,0:T(1,128)S(1)}, s32[1,1,1536]{2,1,0:T(1,128)}, u32[]{:S(2)}) copy-start(s32[1,1,1536]{2,1,0:T(1,128)} %param.21) | copy-start | bytes 18436
  19.7 38.8 %all-to-all-start = ((bf16[640,2,128]{2,1,0:T(2,128)(2,1)}), bf16[640,2,128]{2,1,0:T(2,128)(2,1)S(1)}, u32[]{:S(2)}, u32[]{:S(2)}) async-start(bf16[640,2,128]{2,1,0:T(2,128)(2,1)} %bitcast.7), calls=%async_computation | async-start | bytes 655360 | tf_op jit(solution)/shard_map/all_to_all | solution.py:359
  43.1 0.7 copy-start.10
  44.0 0.7 copy-start.4
  44.8 0.7 copy-start.5
  45.5 0.7 copy-start.6
  46.3 0.7 copy-start.9
  66.2 16.2 %copy-start.7 = (bf16[1,96,96]{2,1,0:T(8,128)(2,1)S(1)}, bf16[1,96,96]{2,1,0:T(8,128)(2,1)}, u32[]{:S(2)}) copy-start(bf16[1,96,96]{2,1,0:T(8,128)(2,1)} %param.26) | copy-start | bytes 55300
  66.2 31.6 %all-to-all-start.1 = ((bf16[640,2,128]{2,1,0:T(2,128)(2,1)}), bf16[640,2,128]{2,1,0:T(2,128)(2,1)S(1)}, u32[]{:S(2)}, u32[]{:S(2)}) async-start(bf16[640,2,128]{2,1,0:T(2,128)(2,1)} %bitcast.12), calls=%async_computation.1 | async-start | bytes 655360 | tf_op jit(solution)/shard_map/all_to_all | solution.py:359
